TPU v7x, 256 devices: a whole 4x4x8 slice. The times are simulated.
256 devices in a mesh: gx: 16 (over z, y_lo), gy: 4 (over x), gz: 4 (over y_hi, core).
Axes of the slice: x: 4, y: 4 (y_hi: 2, y_lo: 2; y = y_hi * 2 + y_lo), z: 8, core: 2. Of those that a mesh axis runs over, the one named last changes fastest.
Arguments:
- pressure_start: float32 [256, 256, 1024], P('gx', 'gy', 'gz'), may hold values from -6 to 6
- source: float32 [256, 256, 1024], P('gx', 'gy', 'gz'), may hold values from -16 to 16
- permeability: float32 [256, 256, 1024], P('gx', 'gy', 'gz'), may hold values from 0.1 to 10
Outputs:
- pressure: float32 [256, 256, 1024], P('gx', 'gy', 'gz')
All inputs are finite; a program needn't handle non-finite values.
Results may differ from a plain program's by a relative error of at most 0.0003.
Values sent between devices are 32-bit elements; how exact they have to be, the bound alone decides.
A program may use at most 128 MiB of HBM per device.

v0:
```python
import jax
import jax.numpy as jnp
from jax import lax
from jax.sharding import PartitionSpec as P

RATIO = 8
SWEEPS = 4
COARSE_SWEEPS = 8


OMEGA = 0.8
OMEGA_COARSE = 0.8


def padded_2(block, sides, width):
    for axis, dim in sides:
        count = lax.axis_size(axis)
        forward = [(i, i + 1) for i in range(count - 1)]
        backward = [(target, source) for source, target in forward]
        low = lax.ppermute(
            lax.slice_in_dim(block, block.shape[dim] - width, None, axis=dim), axis, forward
        )
        high = lax.ppermute(lax.slice_in_dim(block, 0, width, axis=dim), axis, backward)
        block = jnp.concatenate([low, block, high], axis=dim)
    return block


def neighbours(padded):
    return (
        padded[:-2, 1:-1, 1:-1],
        padded[2:, 1:-1, 1:-1],
        padded[1:-1, :-2, 1:-1],
        padded[1:-1, 2:, 1:-1],
        padded[1:-1, 1:-1, :-2],
        padded[1:-1, 1:-1, 2:],
    )


def face_weights(padded):
    center = padded[1:-1, 1:-1, 1:-1]
    weights = tuple(
        (
            jnp.where(beside_cell > 0.0, 0.5 * (center + beside_cell), center)
            for beside_cell in neighbours(padded)
        )
    )
    diagonal_sum = weights[0] + weights[1] + weights[2] + weights[3] + weights[4] + weights[5]
    return (weights, diagonal_sum)


def apply_operator(padded, weights, diagonal_sum):
    beside = neighbours(padded)
    flux = weights[0] * beside[0] + weights[1] * beside[1] + weights[2] * beside[2]
    flux = flux + weights[3] * beside[3] + weights[4] * beside[4] + weights[5] * beside[5]
    return diagonal_sum * padded[1:-1, 1:-1, 1:-1] - flux


def block_sum(values):
    depth, rows, width = values.shape
    return values.reshape(depth // RATIO, RATIO, rows // RATIO, RATIO, width // RATIO, RATIO).sum(
        axis=(1, 3, 5)
    )


def coarse_faces(weights):
    depth, rows, width = weights[0].shape
    cells_z, cells_y, cells_x = (depth // RATIO, rows // RATIO, width // RATIO)
    low_z = weights[0][0::RATIO].reshape(cells_z, cells_y, RATIO, cells_x, RATIO).sum(axis=(2, 4))
    high_z = (
        weights[1][RATIO - 1 :: RATIO]
        .reshape(cells_z, cells_y, RATIO, cells_x, RATIO)
        .sum(axis=(2, 4))
    )
    low_y = (
        weights[2][:, 0::RATIO, :].reshape(cells_z, RATIO, cells_y, cells_x, RATIO).sum(axis=(1, 4))
    )
    high_y = (
        weights[3][:, RATIO - 1 :: RATIO, :]
        .reshape(cells_z, RATIO, cells_y, cells_x, RATIO)
        .sum(axis=(1, 4))
    )
    low_x = (
        weights[4][:, :, 0::RATIO].reshape(cells_z, RATIO, cells_y, RATIO, cells_x).sum(axis=(1, 3))
    )
    high_x = (
        weights[5][:, :, RATIO - 1 :: RATIO]
        .reshape(cells_z, RATIO, cells_y, RATIO, cells_x)
        .sum(axis=(1, 3))
    )
    return (low_z, high_z, low_y, high_y, low_x, high_x)


def fine_rims(values):
    return padded_2(values, (("gx", 0), ("gy", 1), ("gz", 2)), 1)


def zero_rims(values):
    return jnp.pad(values, 1)


def coarse_sweeps(coarse_rhs, faces, diagonal_sum, extend):
    correction = OMEGA_COARSE * coarse_rhs / diagonal_sum
    for sweep_index in range(COARSE_SWEEPS - 1):
        applied = apply_operator(extend(correction), faces, diagonal_sum)
        correction = correction + OMEGA_COARSE * (coarse_rhs - applied) / diagonal_sum
    applied = apply_operator(extend(correction), faces, diagonal_sum)
    return (correction, jnp.sum(coarse_rhs - applied), jnp.sum(diagonal_sum))


def shifted_down(values, axis_number):
    upper = lax.slice_in_dim(values, 1, values.shape[axis_number], 1, axis_number)
    empty = jnp.zeros_like(lax.slice_in_dim(values, 0, 1, 1, axis_number))
    return jnp.concatenate((upper, empty), axis=axis_number)


def shards(pressure_start, source, permeability):
    perm_padded = padded_2(permeability, (("gx", 0), ("gy", 1), ("gz", 2)), 1)
    own_weights, diagonal_sum = face_weights(perm_padded)
    applied = apply_operator(fine_rims(pressure_start), own_weights, diagonal_sum)
    start_residual = source - applied
    pressure_now = pressure_start + OMEGA * start_residual / diagonal_sum
    for sweep_index in range(SWEEPS - 1):
        applied = apply_operator(fine_rims(pressure_now), own_weights, diagonal_sum)
        pressure_now = pressure_now + OMEGA * (source - applied) / diagonal_sum
    coarse_rhs = block_sum(start_residual)
    faces = coarse_faces(own_weights)
    coarse_diagonal = faces[0] + faces[1] + faces[2] + faces[3] + faces[4] + faces[5]
    cells_z, cells_y, cells_x = coarse_rhs.shape
    packed = jnp.stack((coarse_rhs, coarse_diagonal, faces[0], faces[2], faces[4])).reshape(1, -1)
    everything = lax.all_gather(packed, ("gx", "gy", "gz"), axis=0, tiled=True)
    count_z, count_y, count_x = (lax.axis_size("gx"), lax.axis_size("gy"), lax.axis_size("gz"))
    coarse_grid = everything.reshape(count_z, count_y, count_x, 5, cells_z, cells_y, cells_x)
    coarse_grid = coarse_grid.transpose(3, 0, 4, 1, 5, 2, 6).reshape(
        5, count_z * cells_z, count_y * cells_y, count_x * cells_x
    )
    rhs_all, diagonal_all = (coarse_grid[0], coarse_grid[1])
    low_z, low_y, low_x = (coarse_grid[2], coarse_grid[3], coarse_grid[4])
    faces_all = (
        low_z,
        shifted_down(low_z, 0),
        low_y,
        shifted_down(low_y, 1),
        low_x,
        shifted_down(low_x, 2),
    )
    correction_all, leftover, diag_total = coarse_sweeps(
        rhs_all, faces_all, diagonal_all, zero_rims
    )
    start_z = lax.axis_index("gx") * cells_z
    start_y = lax.axis_index("gy") * cells_y
    start_x = lax.axis_index("gz") * cells_x
    correction = lax.dynamic_slice(
        correction_all, (start_z, start_y, start_x), (cells_z, cells_y, cells_x)
    )
    correction = correction + leftover / diag_total
    depth_all, rows_all, width_all = pressure_now.shape
    blocks = pressure_now.reshape(cells_z, RATIO, cells_y, RATIO, cells_x, RATIO)
    return (blocks + correction[:, None, :, None, :, None]).reshape(depth_all, rows_all, width_all)


def solution(mesh):
    return jax.shard_map(
        shards,
        mesh=mesh,
        in_specs=(P("gx", "gy", "gz"), P("gx", "gy", "gz"), P("gx", "gy", "gz")),
        out_specs=P("gx", "gy", "gz"),
        check_vma=False,
    )
```

profile of v0, /device:TPU:1, one launch (start us, length us, event | category | flops | bytes accessed | tf_op | source)
XLA Modules:
  0.0 635.9 jit_solution(9319954442190913622)
XLA Ops:
  35.7 4.5 collective-permute-start.10
  51.2 13.1 %divide_add_fusion = (f32[16,64,256]{2,1,0:T(8,128)S(1)}, f32[16,64,256]{2,1,0:T(8,128)}, f32[16,64,256]{2,1,0:T(8,128)}, f32[16,64,256]{2,1,0:T(8,128)}, f32[16...) fusion(f32[16,64,256]{2,1,0:T(8,128)} %param.3, ...), kind=kLoop, calls=%fused_computation.197 | loop fusion | flops 17301504 | bytes 14248512 | tf_op jit(solution)/shard_map/add | solution.py:121
  64.4 12.2 %reshape.81 = f32[2,8,8,8,32,8]{5,4,3,2,1,0:T(8,128)} reshape(f32[16,64,256]{2,1,0:T(8,128)} %get-tuple-element.6) | data formatting | bytes 2097152 | tf_op jit(solution)/shard_map/reshape | solution.py:60
  76.6 7.2 %reduce_sum.93 = f32[2,8,32]{2,1,0:T(8,128)S(1)} reduce(f32[2,8,8,8,32,8]{5,4,3,2,1,0:T(8,128)} %reshape.81, f32[]{:T(128)} %constant.12.clone.1), dimensions={1,3,5}, to_apply=%region_0.1 | reduce | flops 261632 | bytes 1050628 | tf_op jit(solution)/shard_map/reduce_sum | solution.py:60
  83.8 5.4 slice.474
  90.2 5.2 slice.473
  120.4 5.2 collective-permute-start.12
  128.8 5.3 collective-permute-start.14
  138.9 5.9 collective-permute-start.16
  147.1 8.0 %fusion.39 = f32[16,64,256]{2,1,0:T(8,128)S(1)} fusion(f32[16,64,256]{2,1,0:T(8,128)} %copy-done.6, f32[16,64,256]{2,1,0:T(8,128)} %param.4, f32[16,64,256]{2,1,0:T(8,128)S(1)} %get-tuple-element.12, f32[18,66,1]{2,1,0:T(8,128)} %copy.20, f32[18,1,256]{2,1,0:T(1,128)S(1)} %copy-done.11, f32[18,1,256]{2,1,0:T(1,128)S(1)} %copy-done.13, ...), kind=kLoop, calls=%fused_computation.129 | loop fusion | flops 10485760 | bytes 9614624 | tf_op jit(solution)/shard_map/add | solution.py:124
  156.4 4.6 collective-permute-start.18
  164.2 4.6 collective-permute-start.20
  175.7 7.0 %collective-permute-start.22 = (f32[18,66,1]{1,2,0:T(1,128)S(1)}, f32[18,66,1]{1,2,0:T(1,128)S(1)}, u32[]{:S(2)}, u32[]{:S(2)}) collective-permute-start(f32[18,66,1]{1,2,0:T(1,128)S(1)} %copy.21), channel_id=1, source_target_pairs={{0,1},{1,2},{2,3},{4,5},{5,6},{6,7},{8,9},{9,10},{10,11},{12,13},{... | collective-permute-start | bytes 14264 | tf_op jit(solution)/shard_map/ppermute | solution.py:20
  185.1 5.4 fusion.23
  191.9 4.9 collective-permute-start.24
  200.0 4.6 collective-permute-start.26
  208.4 7.0 %collective-permute-start.28 = (f32[18,66,1]{1,2,0:T(1,128)S(1)}, f32[18,66,1]{1,2,0:T(1,128)S(1)}, u32[]{:S(2)}, u32[]{:S(2)}) collective-permute-start(f32[18,66,1]{1,2,0:T(1,128)S(1)} %copy.25), channel_id=1, source_target_pairs={{0,1},{1,2},{2,3},{4,5},{5,6},{6,7},{8,9},{9,10},{10,11},{12,13},{... | collective-permute-start | bytes 14264 | tf_op jit(solution)/shard_map/ppermute | solution.py:20
  217.9 325.2 %all-gather.3.cloned.1.call-done = f32[256,1,2560]{2,1,0:T(1,128)} async-done(((f32[1,1,2560]{2,1,0:T(1,128)}), f32[256,1,2560]{2,1,0:T(1,128)}) %all-gather.3.cloned.1.call-update) | async-done | bytes 2621456 | tf_op jit(solution)/shard_map/all_gather | solution.py:130
  543.1 8.0 %reduce.1 = f32[256,2560]{1,0:T(8,128)S(1)} reduce(f32[256,1,2560]{2,1,0:T(1,128)} %all-gather.3.cloned.1.call-done, f32[]{:T(128)} %constant.56), dimensions={1}, to_apply=%all-gather.reduce_sub_computation | reduce | bytes 5242884 | tf_op jit(solution)/shard_map/all_gather | solution.py:130
  551.0 5.5 reshape.89
  556.6 8.3 %slice_reduce_fusion = (f32[]{:T(128)}, f32[1,16,2,4,8,4,32]{6,4,2,0,5,3,1:T(8,128)}, f32[1,16,2,4,8,4,32]{6,4,2,0,5,3,1:T(8,128)}, f32[1,16,2,4,8,4,32]{6,4,2,0...) fusion(f32[5,16,2,4,8,4,32]{6,4,2,0,5,3,1:T(8,128)} %bitcast.34), kind=kLoop, calls=%fused_computation.356 | loop fusion | flops 131071 | bytes 5242884 | tf_op jit(solution)/shard_map/reduce_sum | solution.py:107
  600.7 8.0 %add.436 = f32[2,8,8,8,32,8]{5,4,3,2,1,0:T(8,128)} broadcast(f32[2,8,32]{2,1,0:T(8,128)S(1)} %dynamic-slice_add_fusion), dimensions={0,2,4} | broadcast | bytes 1050624 | tf_op jit(solution)/shard_map/add | solution.py:158
  608.7 13.7 %add.437 = f32[16,64,256]{2,1,0:T(8,128)} reshape(f32[2,8,8,8,32,8]{5,4,3,2,1,0:T(8,128)} %add.436) | data formatting | bytes 2097152 | tf_op jit(solution)/shard_map/add | solution.py:158
  622.4 6.4 %fusion.7 = f32[16,64,256]{2,1,0:T(8,128)} fusion(f32[16,64,256]{2,1,0:T(8,128)} %add.437, f32[16,64,256]{2,1,0:T(8,128)S(1)} %copy-done.5, f32[16,64,256]{2,1,0:T(8,128)} %param.4, f32[16,64,256]{2,1,0:T(8,128)S(1)} %copy-done.3, f32[18,66,1]{2,1,0:T(8,128)} %copy.28, f32[18,1,256]{2,1,0:T(1,128)S(1)} %collective-permute-done.27, ...), kind=kLoop, calls=%fused_computation.61 | loop fusion | flops 10747904 | bytes 10663200 | tf_op jit(solution)/shard_map/add | solution.py:158
  (169 shorter events, 134.9 us)
Async XLA Ops:
  6.5 536.5 %all-gather.3.cloned.1.call-start = ((), (), s32[]{:S(2)}) async-start(), calls=%async_computation | async-start | bytes 2631680 | tf_op jit(solution)/shard_map/all_gather | solution.py:130
  7.4 11.7 %collective-permute-start.6 = (f32[1,64,256]{2,1,0:T(8,128)S(1)}, f32[1,64,256]{2,1,0:T(8,128)S(1)}, u32[]{:S(2)}, u32[]{:S(2)}) collective-permute-start(f32[1,64,256]{2,1,0:T(8,128)S(1)} %get-tuple-element.48), channel_id=1, source_target_pairs={{0,16},{16,32},{32,48},{48,64},{64,80},{80,96},{96,112},{112,128},... | collective-permute-start | bytes 196616 | tf_op jit(solution)/shard_map/ppermute | solution.py:20
  11.4 9.0 %collective-permute-start.7 = (f32[1,64,256]{2,1,0:T(8,128)S(1)}, f32[1,64,256]{2,1,0:T(8,128)S(1)}, u32[]{:S(2)}, u32[]{:S(2)}) collective-permute-start(f32[1,64,256]{2,1,0:T(8,128)S(1)} %get-tuple-element.47), channel_id=1, source_target_pairs={{16,0},{32,16},{48,32},{64,48},{80,64},{96,80},{112,96},{128,112},... | collective-permute-start | bytes 196616 | tf_op jit(solution)/shard_map/ppermute | solution.py:23
  13.6 12.2 %collective-permute-start = (f32[1,64,256]{2,1,0:T(8,128)S(1)}, f32[1,64,256]{2,1,0:T(8,128)S(1)}, u32[]{:S(2)}, u32[]{:S(2)}) collective-permute-start(f32[1,64,256]{2,1,0:T(8,128)S(1)} %get-tuple-element.46), channel_id=1, source_target_pairs={{0,16},{16,32},{32,48},{48,64},{64,80},{80,96},{96,112},{112,128},... | collective-permute-start | bytes 196616 | tf_op jit(solution)/shard_map/ppermute | solution.py:20
  17.8 8.2 %collective-permute-start.1 = (f32[1,64,256]{2,1,0:T(8,128)S(1)}, f32[1,64,256]{2,1,0:T(8,128)S(1)}, u32[]{:S(2)}, u32[]{:S(2)}) collective-permute-start(f32[1,64,256]{2,1,0:T(8,128)S(1)} %get-tuple-element.45), channel_id=1, source_target_pairs={{16,0},{32,16},{48,32},{64,48},{80,64},{96,80},{112,96},{128,112},... | collective-permute-start | bytes 196616 | tf_op jit(solution)/shard_map/ppermute | solution.py:23
  20.6 9.9 %collective-permute-start.9 = (f32[18,1,256]{2,1,0:T(1,128)S(1)}, f32[18,1,256]{2,1,0:T(1,128)S(1)}, u32[]{:S(2)}, u32[]{:S(2)}) collective-permute-start(f32[18,1,256]{2,1,0:T(1,128)S(1)} %get-tuple-element.38), channel_id=1, source_target_pairs={{4,0},{8,4},{12,8},{5,1},{9,5},{13,9},{6,2},{10,6},{14,10},{7,3},{... | collective-permute-start | bytes 55304 | tf_op jit(solution)/shard_map/ppermute | solution.py:23
  21.9 8.6 %collective-permute-start.8 = (f32[18,1,256]{2,1,0:T(1,128)S(1)}, f32[18,1,256]{2,1,0:T(1,128)S(1)}, u32[]{:S(2)}, u32[]{:S(2)}) collective-permute-start(f32[18,1,256]{2,1,0:T(1,128)S(1)} %get-tuple-element.37), channel_id=1, source_target_pairs={{0,4},{4,8},{8,12},{1,5},{5,9},{9,13},{2,6},{6,10},{10,14},{3,7},{... | collective-permute-start | bytes 55304 | tf_op jit(solution)/shard_map/ppermute | solution.py:20
  26.1 14.1 %collective-permute-start.2 = (f32[18,1,256]{2,1,0:T(1,128)S(1)}, f32[18,1,256]{2,1,0:T(1,128)S(1)}, u32[]{:S(2)}, u32[]{:S(2)}) collective-permute-start(f32[18,1,256]{2,1,0:T(1,128)S(1)} %get-tuple-element.36), channel_id=1, source_target_pairs={{0,4},{4,8},{8,12},{1,5},{5,9},{9,13},{2,6},{6,10},{10,14},{3,7},{... | collective-permute-start | bytes 55304 | tf_op jit(solution)/shard_map/ppermute | solution.py:20
  29.2 11.0 %collective-permute-start.3 = (f32[18,1,256]{2,1,0:T(1,128)S(1)}, f32[18,1,256]{2,1,0:T(1,128)S(1)}, u32[]{:S(2)}, u32[]{:S(2)}) collective-permute-start(f32[18,1,256]{2,1,0:T(1,128)S(1)} %get-tuple-element.35), channel_id=1, source_target_pairs={{4,0},{8,4},{12,8},{5,1},{9,5},{13,9},{6,2},{10,6},{14,10},{7,3},{... | collective-permute-start | bytes 55304 | tf_op jit(solution)/shard_map/ppermute | solution.py:23
  31.2 14.5 %collective-permute-start.11 = (f32[18,66,1]{1,2,0:T(1,128)S(1)}, f32[18,66,1]{1,2,0:T(1,128)S(1)}, u32[]{:S(2)}, u32[]{:S(2)}) collective-permute-start(f32[18,66,1]{1,2,0:T(1,128)S(1)} %copy.15), channel_id=1, source_target_pairs={{1,0},{2,1},{3,2},{5,4},{6,5},{7,6},{9,8},{10,9},{11,10},{13,12},{... | collective-permute-start | bytes 14264 | tf_op jit(solution)/shard_map/ppermute | solution.py:23
  35.7 11.2 %collective-permute-start.10 = (f32[18,66,1]{1,2,0:T(1,128)S(1)}, f32[18,66,1]{1,2,0:T(1,128)S(1)}, u32[]{:S(2)}, u32[]{:S(2)}) collective-permute-start(f32[18,66,1]{1,2,0:T(1,128)S(1)} %copy.13), channel_id=1, source_target_pairs={{0,1},{1,2},{2,3},{4,5},{5,6},{6,7},{8,9},{9,10},{10,11},{12,13},{... | collective-permute-start | bytes 14264 | tf_op jit(solution)/shard_map/ppermute | solution.py:20
  40.9 7.1 %collective-permute-start.4 = (f32[18,66,1]{1,2,0:T(1,128)S(1)}, f32[18,66,1]{1,2,0:T(1,128)S(1)}, u32[]{:S(2)}, u32[]{:S(2)}) collective-permute-start(f32[18,66,1]{1,2,0:T(1,128)S(1)} %copy.9), channel_id=1, source_target_pairs={{0,1},{1,2},{2,3},{4,5},{5,6},{6,7},{8,9},{9,10},{10,11},{12,13},{... | collective-permute-start | bytes 14264 | tf_op jit(solution)/shard_map/ppermute | solution.py:20
  43.6 6.5 %collective-permute-start.5 = (f32[18,66,1]{1,2,0:T(1,128)S(1)}, f32[18,66,1]{1,2,0:T(1,128)S(1)}, u32[]{:S(2)}, u32[]{:S(2)}) collective-permute-start(f32[18,66,1]{1,2,0:T(1,128)S(1)} %copy.11), channel_id=1, source_target_pairs={{1,0},{2,1},{3,2},{5,4},{6,5},{7,6},{9,8},{10,9},{11,10},{13,12},{... | collective-permute-start | bytes 14264 | tf_op jit(solution)/shard_map/ppermute | solution.py:23
  119.1 6.5 %collective-permute-start.13 = (f32[1,64,256]{2,1,0:T(8,128)S(1)}, f32[1,64,256]{2,1,0:T(8,128)S(1)}, u32[]{:S(2)}, u32[]{:S(2)}) collective-permute-start(f32[1,64,256]{2,1,0:T(8,128)S(1)} %get-tuple-element.44), channel_id=1, source_target_pairs={{16,0},{32,16},{48,32},{64,48},{80,64},{96,80},{112,96},{128,112},... | collective-permute-start | bytes 196616 | tf_op jit(solution)/shard_map/ppermute | solution.py:23
  120.4 7.0 %collective-permute-start.12 = (f32[1,64,256]{2,1,0:T(8,128)S(1)}, f32[1,64,256]{2,1,0:T(8,128)S(1)}, u32[]{:S(2)}, u32[]{:S(2)}) collective-permute-start(f32[1,64,256]{2,1,0:T(8,128)S(1)} %get-tuple-element.43), channel_id=1, source_target_pairs={{0,16},{16,32},{32,48},{48,64},{64,80},{80,96},{96,112},{112,128},... | collective-permute-start | bytes 196616 | tf_op jit(solution)/shard_map/ppermute | solution.py:20
  127.5 6.6 %collective-permute-start.15 = (f32[18,1,256]{2,1,0:T(1,128)S(1)}, f32[18,1,256]{2,1,0:T(1,128)S(1)}, u32[]{:S(2)}, u32[]{:S(2)}) collective-permute-start(f32[18,1,256]{2,1,0:T(1,128)S(1)} %get-tuple-element.34), channel_id=1, source_target_pairs={{4,0},{8,4},{12,8},{5,1},{9,5},{13,9},{6,2},{10,6},{14,10},{7,3},{... | collective-permute-start | bytes 55304 | tf_op jit(solution)/shard_map/ppermute | solution.py:23
  136.6 8.2 %collective-permute-start.17 = (f32[18,66,1]{1,2,0:T(1,128)}, f32[18,66,1]{1,2,0:T(1,128)S(1)}, u32[]{:S(2)}, u32[]{:S(2)}) collective-permute-start(f32[18,66,1]{1,2,0:T(1,128)} %copy.19), channel_id=1, source_target_pairs={{1,0},{2,1},{3,2},{5,4},{6,5},{7,6},{9,8},{10,9},{11,10},{13,12},{... | collective-permute-start | bytes 14264 | tf_op jit(solution)/shard_map/ppermute | solution.py:23
  138.9 7.1 %collective-permute-start.16 = (f32[18,66,1]{1,2,0:T(1,128)S(1)}, f32[18,66,1]{1,2,0:T(1,128)S(1)}, u32[]{:S(2)}, u32[]{:S(2)}) collective-permute-start(f32[18,66,1]{1,2,0:T(1,128)S(1)} %copy.17), channel_id=1, source_target_pairs={{0,1},{1,2},{2,3},{4,5},{5,6},{6,7},{8,9},{9,10},{10,11},{12,13},{... | collective-permute-start | bytes 14264 | tf_op jit(solution)/shard_map/ppermute | solution.py:20
  156.4 6.5 %collective-permute-start.18 = (f32[1,64,256]{2,1,0:T(8,128)S(1)}, f32[1,64,256]{2,1,0:T(8,128)S(1)}, u32[]{:S(2)}, u32[]{:S(2)}) collective-permute-start(f32[1,64,256]{2,1,0:T(8,128)S(1)} %get-tuple-element.41), channel_id=1, source_target_pairs={{0,16},{16,32},{32,48},{48,64},{64,80},{80,96},{96,112},{112,128},... | collective-permute-start | bytes 196616 | tf_op jit(solution)/shard_map/ppermute | solution.py:20
  172.4 10.4 %collective-permute-start.23 = (f32[18,66,1]{1,2,0:T(1,128)S(1)}, f32[18,66,1]{1,2,0:T(1,128)S(1)}, u32[]{:S(2)}, u32[]{:S(2)}) collective-permute-start(f32[18,66,1]{1,2,0:T(1,128)S(1)} %copy.23), channel_id=1, source_target_pairs={{1,0},{2,1},{3,2},{5,4},{6,5},{7,6},{9,8},{10,9},{11,10},{13,12},{... | collective-permute-start | bytes 14264 | tf_op jit(solution)/shard_map/ppermute | solution.py:23
  175.7 8.2 %collective-permute-start.22 = (f32[18,66,1]{1,2,0:T(1,128)S(1)}, f32[18,66,1]{1,2,0:T(1,128)S(1)}, u32[]{:S(2)}, u32[]{:S(2)}) collective-permute-start(f32[18,66,1]{1,2,0:T(1,128)S(1)} %copy.21), channel_id=1, source_target_pairs={{0,1},{1,2},{2,3},{4,5},{5,6},{6,7},{8,9},{9,10},{10,11},{12,13},{... | collective-permute-start | bytes 14264 | tf_op jit(solution)/shard_map/ppermute | solution.py:20
  191.9 6.8 %collective-permute-start.24 = (f32[1,64,256]{2,1,0:T(8,128)S(1)}, f32[1,64,256]{2,1,0:T(8,128)S(1)}, u32[]{:S(2)}, u32[]{:S(2)}) collective-permute-start(f32[1,64,256]{2,1,0:T(8,128)S(1)} %get-tuple-element.39), channel_id=1, source_target_pairs={{0,16},{16,32},{32,48},{48,64},{64,80},{80,96},{96,112},{112,128},... | collective-permute-start | bytes 196616 | tf_op jit(solution)/shard_map/ppermute | solution.py:20
  206.2 9.3 %collective-permute-start.29 = (f32[18,66,1]{1,2,0:T(1,128)S(1)}, f32[18,66,1]{1,2,0:T(1,128)S(1)}, u32[]{:S(2)}, u32[]{:S(2)}) collective-permute-start(f32[18,66,1]{1,2,0:T(1,128)S(1)} %copy.27), channel_id=1, source_target_pairs={{1,0},{2,1},{3,2},{5,4},{6,5},{7,6},{9,8},{10,9},{11,10},{13,12},{... | collective-permute-start | bytes 14264 | tf_op jit(solution)/shard_map/ppermute | solution.py:23
  208.4 8.3 %collective-permute-start.28 = (f32[18,66,1]{1,2,0:T(1,128)S(1)}, f32[18,66,1]{1,2,0:T(1,128)S(1)}, u32[]{:S(2)}, u32[]{:S(2)}) collective-permute-start(f32[18,66,1]{1,2,0:T(1,128)S(1)} %copy.25), channel_id=1, source_target_pairs={{0,1},{1,2},{2,3},{4,5},{5,6},{6,7},{8,9},{9,10},{10,11},{12,13},{... | collective-permute-start | bytes 14264 | tf_op jit(solution)/shard_map/ppermute | solution.py:20
  (21 other events, 467.5 us)
Sparse Core Ops, SparseCore 0:
  119.2 423.8 all-gather.2
where the time goes:
time: 641 us; the launch traced here: 636 us
  waiting for transfers between devices  334 us (52%)
  local copies, waits for them, and re-layouts  117 us (18%)
  starting transfers between devices  96.5 us (15%)
  other arithmetic  73 us (11%)
  between operations  15.8 us (2%)
    all_gather x1, waiting for transfers between devices, shards(): everything = lax.all_gather(packed, ('gx', 'gy', 'gz'), axis=0, tiled=True)  325 us
    ppermute x15, starting transfers between devices, padded_2(): lax.ppermute(lax.slice_in_dim(block, block.shape[dim] - width, None, axis...  71.3 us
    ppermute x15, starting transfers between devices, padded_2(): lax.ppermute(lax.slice_in_dim(block, 0, width, axis=dim), axis, backward)  25.1 us
    add x2, local copies, waits for them, and re-layouts, shards(): blocks + correction[:, None, :, None, :, None]  21.7 us
    add x2, other arithmetic, shards(): pressure_now = pressure_now + OMEGA * (source - applied) / diagonal_sum  13.4 us
    add x1, other arithmetic, shards(): pressure_now = pressure_start + OMEGA * start_residual / diagonal_sum  13.1 us
  transfers between devices with their start and end apart: 31, of which 8 were waited for; matrix products, arithmetic and copies ran while one was open for 5% of the time, Pallas kernels for 0%

commit v1 on v0

v1 whole, which is shorter than its diff:
```python
import jax
import jax.numpy as jnp
from jax import lax
from jax.experimental import pallas as pl
from jax.experimental.pallas import tpu as pltpu
from jax.sharding import PartitionSpec as P

RATIO = 8
SWEEPS = 4
COARSE_SWEEPS = 8
OMEGA = 0.8
MESH = pl.DeviceIdType.MESH

D, R, W = 16, 64, 256
T = R // RATIO
H = W // 2
SLOT = 64
FIRST = 8
CX = W // RATIO
KF = 0


def iota(shape, axis):
    return lax.broadcasted_iota(jnp.int32, shape, axis)


def kernel(
    nx, ny, nz,
    p_hbm, s_hbm, k_hbm, out,
    kx, p0, p1, p2, p3, src, wz, wyl, wyh, wxl, wxh, dia, dinv,
    ysend, yrecv, xsend, xrecv, accs, ebuf, erecv, part1, part2,
    load_sem, fsend, frecv, csend, crecv, a1send, a1recv, a2send, a2recv,
):
    ix, iy, iz = lax.axis_index("gx"), lax.axis_index("gy"), lax.axis_index("gz")
    dirs = (
        ("gx", ix - 1, ix > 0), ("gx", ix + 1, ix < nx - 1),
        ("gy", iy - 1, iy > 0), ("gy", iy + 1, iy < ny - 1),
        ("gz", iz - 1, iz > 0), ("gz", iz + 1, iz < nz - 1),
    )
    press = (p0, p1, p2, p3)
    plane_group = ny * nz
    my_plane = iy * nz + iz

    loads = [
        pltpu.make_async_copy(k_hbm, kx.at[pl.ds(1, D)], load_sem.at[0]),
        pltpu.make_async_copy(p_hbm, p0.at[pl.ds(1, D)], load_sem.at[1]),
        pltpu.make_async_copy(s_hbm, src, load_sem.at[2]),
    ]
    for load in loads:
        load.start()

    barrier = pltpu.get_barrier_semaphore()

    def plane_peer(step):
        other = lax.rem(my_plane + step, plane_group)
        return {"gy": other // nz, "gz": lax.rem(other, nz)}, other

    def line_peer(step):
        other = lax.rem(ix + step, nx)
        return {"gx": other}, other

    for axis, other, exists in dirs:
        @pl.when(exists)
        def _():
            pl.semaphore_signal(barrier, 1, device_id={axis: other}, device_id_type=MESH)

    @pl.loop(1, plane_group)
    def _(step):
        pl.semaphore_signal(barrier, 1, device_id=plane_peer(step)[0], device_id_type=MESH)

    @pl.loop(1, nx)
    def _(step):
        pl.semaphore_signal(barrier, 1, device_id=line_peer(step)[0], device_id_type=MESH)

    near = sum(e.astype(jnp.int32) for _, _, e in dirs)
    lane = iota((1, 128), 1)
    zero_tile = jnp.zeros((8, 128), jnp.float32)

    for d, (_, _, exists) in enumerate(dirs):
        @pl.when(jnp.logical_not(exists))
        def _():
            for f in range(1, 5):
                if d < 2:
                    press[f - 1][d * (D + 1)] = jnp.zeros((R, W), jnp.float32)
                elif d < 4:
                    yrecv[f, d - 2] = jnp.zeros((2, D, H), jnp.float32)
                else:
                    xrecv[f, d - 4] = zero_tile
            for r in range(COARSE_SWEEPS - 1):
                erecv[r, d] = zero_tile

    accs[...] = jnp.zeros(accs.shape, jnp.float32)

    def fine_copy(f, d, incoming=False):
        axis, other, _ = dirs[d]
        end = d ^ 1
        if d < 2:
            field = kx if f == KF else press[f - 1]
            here = field.at[1 if d == 0 else D]
            there = field.at[D + 1 if d == 0 else 0]
            back = field.at[0 if d == 0 else D + 1]
        elif d < 4:
            here, there, back = ysend.at[f, d - 2], yrecv.at[f, end - 2], yrecv.at[f, d - 2]
        else:
            here, there, back = xsend.at[f, d - 4], xrecv.at[f, end - 4], xrecv.at[f, d - 4]
        return pltpu.make_async_remote_copy(
            src_ref=here,
            dst_ref=back if incoming else there,
            send_sem=fsend.at[f, d],
            recv_sem=frecv.at[f, d if incoming else end],
            device_id={axis: other},
            device_id_type=MESH,
        )

    def coarse_copy(r, d, incoming=False):
        axis, other, _ = dirs[d]
        return pltpu.make_async_remote_copy(
            src_ref=ebuf.at[r],
            dst_ref=erecv.at[r, d if incoming else d ^ 1],
            send_sem=csend.at[r, d],
            recv_sem=crecv.at[r, d if incoming else d ^ 1],
            device_id={axis: other},
            device_id_type=MESH,
        )

    def start(make, f, which):
        for d in which:
            @pl.when(dirs[d][2])
            def _():
                make(f, d).start()

    def arrive(make, f, which):
        for d in which:
            @pl.when(dirs[d][2])
            def _():
                make(f, d, True).wait_recv()

    def pack_x(left, right, z, low, high):
        a = zero_tile
        b = zero_tile
        for t in range(T):
            rows = slice(8 * t, 8 * t + 8)
            a = jnp.where(lane == 16 * t, pltpu.roll(left[rows], 16 * t, 1) if t else left[rows], a)
            b = jnp.where(lane == 16 * t, pltpu.roll(right[rows], 16 * t + 1, 1), b)
        a = pltpu.roll(a, z, 1)
        b = pltpu.roll(b, z, 1)
        mine = lax.rem(lane, 16) == z
        return jnp.where(mine, a, low), jnp.where(mine, b, high)

    def unpack_x(f, z):
        back = lax.rem(128 - z, 128)
        low = pltpu.roll(xrecv[f, 0], back, 1)
        high = pltpu.roll(xrecv[f, 1], back, 1)
        lows = [pltpu.roll(low, 128 - 16 * t, 1) if t else low for t in range(T)]
        highs = [pltpu.roll(high, 127 - 16 * t, 1) for t in range(T)]
        return jnp.concatenate(lows, 0), jnp.concatenate(highs, 0)

    row = iota((R, 1), 0)

    def beside(left, right, f, z):
        ylo = [yrecv[f, 0, h, pl.ds(z, 1), :] for h in range(2)]
        yhi = [yrecv[f, 1, h, pl.ds(z, 1), :] for h in range(2)]
        xlo, xhi = unpack_x(f, z)
        low_y = [
            jnp.where(row == 0, g, pltpu.roll(v, 1, 0))
            for v, g in ((left, ylo[0]), (right, ylo[1]))
        ]
        high_y = [
            jnp.where(row == R - 1, g, pltpu.roll(v, R - 1, 0))
            for v, g in ((left, yhi[0]), (right, yhi[1]))
        ]
        rl, rr = pltpu.roll(left, 1, 1), pltpu.roll(right, 1, 1)
        low_x = [jnp.where(lane == 0, xlo, rl), jnp.where(lane == 0, rl, rr)]
        sl, sr = pltpu.roll(left, H - 1, 1), pltpu.roll(right, H - 1, 1)
        high_x = [jnp.where(lane == H - 1, sr, sl), jnp.where(lane == H - 1, xhi, sr)]
        return low_y, high_y, low_x, high_x

    def keep_faces(f, z, halves, low, high):
        for h, v in enumerate(halves):
            ysend[f, 0, h, pl.ds(z, 1), :] = v[0:1]
            ysend[f, 1, h, pl.ds(z, 1), :] = v[R - 1 : R]
        return pack_x(halves[0], halves[1], z, low, high)

    def keep_packed(f, low, high):
        xsend[f, 0] = low
        xsend[f, 1] = high

    loads[0].wait()
    loads[1].wait()
    pl.semaphore_wait(barrier, near + (plane_group - 1) + (nx - 1))
    start(fine_copy, KF, (0, 1))

    for f, field in ((KF, kx), (1, p0)):
        def pack(z, faces, field=field, f=f):
            return keep_faces(f, z, (field[z + 1, :, :H], field[z + 1, :, H:]), *faces)

        keep_packed(f, *lax.fori_loop(0, D, pack, (zero_tile, zero_tile)))
        start(fine_copy, f, (2, 3, 4, 5))
        if f == KF:
            start(fine_copy, 1, (0, 1))

    for d, (_, _, exists) in enumerate(dirs):
        @pl.when(jnp.logical_not(exists))
        def _():
            if d < 2:
                kx[d * (D + 1)] = kx[1 + d * (D - 1)]
            elif d < 4:
                yrecv[KF, d - 2] = ysend[KF, d - 2]
            else:
                xrecv[KF, d - 4] = xsend[KF, d - 4]

    arrive(fine_copy, KF, range(6))

    def weigh(z, carry):
        halves = (kx[z + 1, :, :H], kx[z + 1, :, H:])
        around = beside(halves[0], halves[1], KF, z)
        c = z // RATIO
        for h in range(2):
            cols = slice(h * H, (h + 1) * H)
            k = halves[h]
            low_z = 0.5 * (k + kx[z, :, cols])
            high_z = 0.5 * (k + kx[z + 2, :, cols])
            faces = [0.5 * (k + g[h]) for g in around]
            wz[z, :, cols] = low_z
            total = low_z + high_z + faces[0] + faces[1] + faces[2] + faces[3]
            for n, (ref, face) in enumerate(zip((wyl, wyh, wxl, wxh), faces)):
                ref[z, :, cols] = face
                accs[1 + n, c, :, cols] += face
            dia[z, :, cols] = total
            dinv[z, :, cols] = OMEGA / total
        return carry

    lax.fori_loop(0, D, weigh, 0)
    wz[D] = 0.5 * (kx[D] + kx[D + 1])
    loads[2].wait()

    def sweep_plane(n, z, faces):
        v_ref = press[n - 1]
        halves = (v_ref[z + 1, :, :H], v_ref[z + 1, :, H:])
        around = beside(halves[0], halves[1], n, z)
        new = []
        for h in range(2):
            cols = slice(h * H, (h + 1) * H)
            v = halves[h]
            flux = wz[z, :, cols] * v_ref[z, :, cols] + wz[z + 1, :, cols] * v_ref[z + 2, :, cols]
            for ref, g in zip((wyl, wyh, wxl, wxh), around):
                flux = flux + ref[z, :, cols] * g[h]
            flux = src[z, :, cols] + flux
            if n == 1:
                accs[0, z // RATIO, :, cols] += flux - dia[z, :, cols] * v
            v = (1.0 - OMEGA) * v + dinv[z, :, cols] * flux
            if n < SWEEPS:
                press[n][z + 1, :, cols] = v
            else:
                out[z, :, cols] = v
            new.append(v)
        if n == SWEEPS:
            return faces
        return keep_faces(n + 1, z, new, *faces)

    def sweep(n):
        arrive(fine_copy, n, range(6))
        faces = (zero_tile, zero_tile)
        faces = lax.fori_loop(
            0, 2, lambda i, fc: sweep_plane(n, i * (D - 1), fc), faces
        )
        faces = lax.fori_loop(1, 3, lambda z, fc: sweep_plane(n, z, fc), faces)
        if n < SWEEPS:
            start(fine_copy, n + 1, (0, 1))
        faces = lax.fori_loop(3, D - 1, lambda z, fc: sweep_plane(n, z, fc), faces)
        if n < SWEEPS:
            keep_packed(n + 1, *faces)
            start(fine_copy, n + 1, (2, 3, 4, 5))

    sweep(1)

    column, spot = iota((W, 128), 0), iota((W, 128), 1)

    def pick(c, offset):
        hit = spot == c * SLOT + FIRST + column // RATIO
        if offset is not None:
            hit = jnp.logical_and(hit, lax.rem(column, RATIO) == offset)
        return jnp.where(hit, 1.0, 0.0).astype(jnp.float32)

    def dot(a, b):
        return jnp.dot(a, b, precision=lax.Precision.HIGHEST, preferred_element_type=jnp.float32)

    def tile_sum(plane):
        return jnp.sum(plane.reshape(T, RATIO, W), axis=1)

    totals = None
    for c in range(2):
        summed = jnp.concatenate(
            [
                tile_sum(accs[0, c]),
                tile_sum(wz[RATIO * c]),
                tile_sum(wz[RATIO * c + RATIO]),
                accs[1, c].reshape(T, RATIO, W)[:, 0],
                accs[2, c].reshape(T, RATIO, W)[:, RATIO - 1],
            ],
            axis=0,
        )
        parts = [
            dot(summed, pick(c, None)),
            dot(tile_sum(accs[3, c]), pick(c, 0)),
            dot(tile_sum(accs[4, c]), pick(c, RATIO - 1)),
        ]
        both = jnp.concatenate(parts, axis=0)
        totals = both if totals is None else totals + both
    rhs, zl, zh, yl, yh, xl, xh = [totals[8 * n : 8 * n + 8] for n in range(7)]
    cdiag = zl + zh + yl + yh + xl + xh
    inside = lax.rem(lane, SLOT)
    valid = jnp.logical_and(inside >= FIRST, inside < FIRST + CX)
    scale = jnp.where(valid, OMEGA / jnp.where(valid, cdiag, 1.0), 0.0)
    fixed = scale * rhs
    sides = [scale * w for w in (zl, zh, yl, yh, xl, xh)]

    tile_row = iota((8, 1), 0)
    even = lane < SLOT
    edges = (
        even, jnp.logical_not(even), tile_row == 0, tile_row == 7,
        inside == FIRST, inside == FIRST + CX - 1,
    )

    def coarse_sweep(r):
        e = ebuf[r]
        arrive(coarse_copy, r, range(6))
        other_plane = pltpu.roll(e, SLOT, 1)
        around = (
            jnp.where(edges[0], pltpu.roll(erecv[r, 0], SLOT, 1), other_plane),
            jnp.where(edges[1], pltpu.roll(erecv[r, 1], SLOT, 1), other_plane),
            jnp.where(edges[2], pltpu.roll(erecv[r, 2], 1, 0), pltpu.roll(e, 1, 0)),
            jnp.where(edges[3], pltpu.roll(erecv[r, 3], 7, 0), pltpu.roll(e, 7, 0)),
            jnp.where(edges[4], pltpu.roll(erecv[r, 4], 128 - (CX - 1), 1), pltpu.roll(e, 1, 1)),
            jnp.where(edges[5], pltpu.roll(erecv[r, 5], CX - 1, 1), pltpu.roll(e, 127, 1)),
        )
        e = (1.0 - OMEGA) * e + fixed
        for w, g in zip(sides, around):
            e = e + w * g
        return e

    def publish(r, e):
        ebuf[r] = e
        if r < COARSE_SWEEPS - 1:
            start(coarse_copy, r, range(6))

    publish(0, fixed)
    for r in range(COARSE_SWEEPS - 1):
        publish(r + 1, coarse_sweep(r))
        if r in (1, 3, 5):
            sweep(2 + r // 2)
    swept = ebuf[COARSE_SWEEPS - 1]

    outside = zero_tile
    for (_, _, exists), edge, w in zip(dirs, edges, (zl, zh, yl, yh, xl, xh)):
        gone = jnp.where(exists, 0.0, 1.0)
        outside = outside + jnp.where(edge, gone * w, 0.0)

    def share(buf, ssem, rsem, count, me, peer_of):
        @pl.loop(1, count)
        def _(step):
            peer, other = peer_of(step)
            pltpu.make_async_remote_copy(
                src_ref=buf.at[me], dst_ref=buf.at[me], send_sem=ssem.at[other],
                recv_sem=rsem.at[me], device_id=peer, device_id_type=MESH,
            ).start()

        def finish():
            @pl.loop(1, count)
            def _(step):
                peer, other = peer_of(step)
                pltpu.make_async_remote_copy(
                    src_ref=buf.at[me], dst_ref=buf.at[other], send_sem=ssem.at[other],
                    recv_sem=rsem.at[other], device_id=peer, device_id_type=MESH,
                ).wait_recv()
            return jnp.sum(buf[...], axis=0)

        def drain():
            @pl.loop(1, count)
            def _(step):
                peer, other = peer_of(step)
                pltpu.make_async_remote_copy(
                    src_ref=buf.at[me], dst_ref=buf.at[me], send_sem=ssem.at[other],
                    recv_sem=rsem.at[me], device_id=peer, device_id_type=MESH,
                ).wait_send()

        return finish, drain

    part1[my_plane, 0] = rhs - outside * swept
    part1[my_plane, 1] = cdiag
    finish1, drain1 = share(part1, a1send, a1recv, plane_group, my_plane, plane_peer)

    spread = [
        lax.dot_general(
            swept, pick(c, None), (((1,), (1,)), ((), ())),
            precision=lax.Precision.HIGHEST, preferred_element_type=jnp.float32,
        )
        for c in range(2)
    ]
    for c in range(2):
        wide = jnp.broadcast_to(spread[c][:, None, :], (T, RATIO, W)).reshape(R, W)
        accs[0, c] = wide

    part2[ix] = finish1()
    finish2, drain2 = share(part2, a2send, a2recv, nx, ix, line_peer)

    def add_spread(z, carry):
        out[z] = out[z] + accs[0, z // RATIO]
        return carry

    lax.fori_loop(0, D, add_spread, 0)

    for f in range(5):
        for d in range(6):
            @pl.when(dirs[d][2])
            def _():
                fine_copy(f, d).wait_send()
    for r in range(COARSE_SWEEPS - 1):
        for d in range(6):
            @pl.when(dirs[d][2])
            def _():
                coarse_copy(r, d).wait_send()
    drain1()

    sums = finish2()
    drain2()
    shift = jnp.sum(sums[0]) / jnp.sum(sums[1])

    def add_shift(z, carry):
        out[z] = out[z] + shift
        return carry

    lax.fori_loop(0, D, add_shift, 0)


def solution(mesh):
    nx, ny, nz = mesh.shape["gx"], mesh.shape["gy"], mesh.shape["gz"]
    f32 = jnp.float32
    dma = pltpu.SemaphoreType.DMA
    rounds = COARSE_SWEEPS - 1

    def body(*refs):
        kernel(nx, ny, nz, *refs)

    def shards(pressure_start, source, permeability):
        block = pltpu.VMEM((D, R, W), f32)
        wide = pltpu.VMEM((D + 2, R, W), f32)
        return pl.pallas_call(
            body,
            out_shape=jax.ShapeDtypeStruct((D, R, W), f32),
            in_specs=[pl.BlockSpec(memory_space=pl.ANY)] * 3,
            out_specs=pl.BlockSpec(memory_space=pltpu.VMEM),
            scratch_shapes=[
                wide, wide, wide, wide, wide,
                block, pltpu.VMEM((D + 1, R, W), f32), block, block, block, block, block, block,
                pltpu.VMEM((5, 2, 2, D, H), f32), pltpu.VMEM((5, 2, 2, D, H), f32),
                pltpu.VMEM((5, 2, 8, 128), f32), pltpu.VMEM((5, 2, 8, 128), f32),
                pltpu.VMEM((5, 2, R, W), f32),
                pltpu.VMEM((COARSE_SWEEPS, 8, 128), f32), pltpu.VMEM((rounds, 6, 8, 128), f32),
                pltpu.VMEM((ny * nz, 2, 8, 128), f32), pltpu.VMEM((nx, 2, 8, 128), f32),
                dma((3,)), dma((5, 6)), dma((5, 6)), dma((rounds, 6)), dma((rounds, 6)),
                dma((ny * nz,)), dma((ny * nz,)), dma((nx,)), dma((nx,)),
            ],
            compiler_params=pltpu.CompilerParams(
                collective_id=0, has_side_effects=True, vmem_limit_bytes=40 << 20
            ),
        )(pressure_start, source, permeability)

    spec = P("gx", "gy", "gz")
    return jax.shard_map(
        shards, mesh=mesh, in_specs=(spec, spec, spec), out_specs=spec, check_vma=False
    )
```

time: 641 us -> 73.1 us (0.11)
  waiting for transfers between devices: 334 us -> 0 us
  local copies, waits for them, and re-layouts: 117 us -> 4.65 us
  starting transfers between devices: 96.5 us -> 0 us
  other arithmetic: 73 us -> 0 us
  Pallas kernels: 0 us -> 67.3 us
  between operations: 15.8 us -> 0.01 us
    all_gather x1 -> x0, waiting for transfers between devices: 325 us -> none  [shards(): everything = lax.all_gather(packed, ('gx', 'gy', 'gz'), axis=0, tiled=True)]
    ppermute x30 -> x0, starting transfers between devices: 96.5 us -> none  [the longest x15 71.3 us: padded_2(): lax.ppermute(lax.slice_in_dim(block, block.shape[dim] - width, None, axis...]
    pallas_call x0 -> x1, Pallas kernels: none -> 67.3 us  [shards(): pl.pallas_call(body, out_shape=jax.ShapeDtypeStruct((D, R, W), f32), in_s...]
    slice x36 -> x0, local copies, waits for them, and re-layouts: 40.3 us -> none  [the longest x3 9.69 us: shards(): low_z, low_y, low_x = (coarse_grid[2], coarse_grid[3], coarse_grid[4])]
    add x12 -> x0, other arithmetic: 37.7 us -> none  [the longest x2 13.4 us: shards(): pressure_now = pressure_now + OMEGA * (source - applied) / diagonal_sum]
    reshape x6 -> x0, local copies, waits for them, and re-layouts: 27.8 us -> none  [the longest x1 12.2 us: block_sum(): values.reshape(depth // RATIO, RATIO, rows // RATIO, RATIO, width // RATI...]
    reduce_sum x9 -> x0, other arithmetic: 26.3 us -> none  [the longest x2 9.57 us: coarse_sweeps(): return (correction, jnp.sum(coarse_rhs - applied), jnp.sum(diagonal_sum))]
    add x2 -> x0, local copies, waits for them, and re-layouts: 21.7 us -> none  [shards(): blocks + correction[:, None, :, None, :, None]]
  transfers between devices with their start and end apart: 31 -> 0, of which waited for: 8 -> 0; matrix products, arithmetic and copies ran while one was open for 5% -> 0% of each run, Pallas kernels for 0% -> 0%
where the time goes in v1:
time: 73.1 us; the launch traced here: 72 us
  Pallas kernels  67.3 us (92%)
  local copies, waits for them, and re-layouts  4.65 us (6%)
    pallas_call x1, Pallas kernels, shards(): pl.pallas_call(body, out_shape=jax.ShapeDtypeStruct((D, R, W), f32), in_s...  67.3 us
    unnamed x7, local copies, waits for them, and re-layouts  4.65 us

profile of v1, /device:TPU:1, one launch (start us, length us, event | category | flops | bytes accessed | tf_op | source)
XLA Modules:
  0.0 72.0 jit_solution(14405558467558923786)
XLA Ops:
  0.0 0.0 copy-start
  0.0 1.2 %copy-done = f32[16,64,256]{2,1,0:T(8,128)S(1)} copy-done((f32[16,64,256]{2,1,0:T(8,128)S(1)}, f32[16,64,256]{2,1,0:T(8,128)}, u32[]{:S(2)}) %copy-start) | copy-done | bytes 1048600
  1.2 0.0 copy-start.1
  1.2 1.2 %copy-done.1 = f32[16,64,256]{2,1,0:T(8,128)S(1)} copy-done((f32[16,64,256]{2,1,0:T(8,128)S(1)}, f32[16,64,256]{2,1,0:T(8,128)}, u32[]{:S(2)}) %copy-start.1) | copy-done | bytes 1048600
  2.5 0.0 copy-start.2
  2.5 1.2 %copy-done.2 = f32[16,64,256]{2,1,0:T(8,128)S(1)} copy-done((f32[16,64,256]{2,1,0:T(8,128)S(1)}, f32[16,64,256]{2,1,0:T(8,128)}, u32[]{:S(2)}) %copy-start.2) | copy-done | bytes 1048600
  3.7 67.3 %shard_map.37 = f32[16,64,256]{2,1,0:T(8,128)S(1)} custom-call(f32[16,64,256]{2,1,0:T(8,128)S(1)} %copy-done, f32[16,64,256]{2,1,0:T(8,128)S(1)} %copy-done.1, f32[16,64,256]{2,1,0:T(8,128)S(1)} %copy-done.2), custom_call_target="tpu_custom_call" | custom-call | tf_op jit(solution)/shard_map/pallas_call | solution.py:448
  71.0 1.0 %copy.5 = f32[16,64,256]{2,1,0:T(8,128)} copy(f32[16,64,256]{2,1,0:T(8,128)S(1)} %shard_map.37) | data formatting | bytes 2097152
Async XLA Ops:
  0.0 1.2 %copy-start = (f32[16,64,256]{2,1,0:T(8,128)S(1)}, f32[16,64,256]{2,1,0:T(8,128)}, u32[]{:S(2)}) copy-start(f32[16,64,256]{2,1,0:T(8,128)} %refs_0_.1) | copy-start | bytes 3145732
  1.2 1.2 %copy-start.1 = (f32[16,64,256]{2,1,0:T(8,128)S(1)}, f32[16,64,256]{2,1,0:T(8,128)}, u32[]{:S(2)}) copy-start(f32[16,64,256]{2,1,0:T(8,128)} %refs_1_.1) | copy-start | bytes 3145732
  2.5 1.2 %copy-start.2 = (f32[16,64,256]{2,1,0:T(8,128)S(1)}, f32[16,64,256]{2,1,0:T(8,128)}, u32[]{:S(2)}) copy-start(f32[16,64,256]{2,1,0:T(8,128)} %refs_2_.1) | copy-start | bytes 3145732

commit v2 on v1

v2 whole, which is shorter than its diff:
```python
import jax
import jax.numpy as jnp
from jax import lax
from jax.experimental import pallas as pl
from jax.experimental.pallas import tpu as pltpu
from jax.sharding import PartitionSpec as P

RATIO = 8
SWEEPS = 4
COARSE_SWEEPS = 8
OMEGA = 0.8
MESH = pl.DeviceIdType.MESH

D, R, W = 16, 64, 256
T = R // RATIO
H = W // 2
TOP = 8
SLOT = 64
FIRST = 8
CX = W // RATIO
REACH = 4
BLOCKS = 2 * REACH + 1
KF = 0
GROUP = 16


def iota(shape, axis):
    return lax.broadcasted_iota(jnp.int32, shape, axis)


def split3(a):
    high = a.astype(jnp.bfloat16)
    rest = a - high.astype(jnp.float32)
    mid = rest.astype(jnp.bfloat16)
    low = (rest - mid.astype(jnp.float32)).astype(jnp.bfloat16)
    return jnp.concatenate([high, mid, low], axis=0)


def select_dot(a, matrix, contract):
    n = a.shape[0]
    b = lax.dot_general(
        split3(a), matrix, (((1,), (contract,)), ((), ())), preferred_element_type=jnp.float32
    )
    return b[:n] + b[n : 2 * n] + b[2 * n :]


def kernel(
    nx, ny, nz,
    p_hbm, s_hbm, k_hbm, out, shift_out,
    kx, p0, p1, p2, p3, src, wz, wyl, wyh, wxl, wxh, dia, dinv, acc, gsum, gpick, corr,
    xsend, xrecv, own_w, xw, zw, yw, own_f, xf, zf, yf, sides, part1, part2,
    load_sem, fsend, frecv, cxs, cxr, czs, czr, cys, cyr, a1send, a1recv, a2send, a2recv,
):
    ix, iy, iz = lax.axis_index("gx"), lax.axis_index("gy"), lax.axis_index("gz")
    dirs = (
        ("gx", ix - 1, ix > 0), ("gx", ix + 1, ix < nx - 1),
        ("gy", iy - 1, iy > 0), ("gy", iy + 1, iy < ny - 1),
        ("gz", iz - 1, iz > 0), ("gz", iz + 1, iz < nz - 1),
    )
    press = (p0, p1, p2, p3)
    plane_group = ny * nz
    my_plane = iy * nz + iz
    own = pl.ds(TOP, R)
    planes = pl.ds(1, D)

    loads = []
    for n, (ref, place) in enumerate(((k_hbm, kx), (p_hbm, p0), (s_hbm, src))):
        for h in range(2):
            there = place.at[h, planes, own] if n < 2 else place.at[h]
            loads.append(
                pltpu.make_async_copy(ref.at[:, :, pl.ds(h * H, H)], there, load_sem.at[n, h])
            )
    for load in loads:
        load.start()

    barrier = pltpu.get_barrier_semaphore()

    def plane_peer(step):
        other = lax.rem(my_plane + step, plane_group)
        return {"gy": other // nz, "gz": lax.rem(other, nz)}, other

    def line_peer(step):
        other = lax.rem(ix + step, nx)
        return {"gx": other}, other

    for axis, other, exists in dirs:
        @pl.when(exists)
        def _():
            pl.semaphore_signal(barrier, 1, device_id={axis: other}, device_id_type=MESH)

    @pl.loop(1, plane_group)
    def _(step):
        pl.semaphore_signal(barrier, 1, device_id=plane_peer(step)[0], device_id_type=MESH)

    @pl.loop(1, nx)
    def _(step):
        pl.semaphore_signal(barrier, 1, device_id=line_peer(step)[0], device_id_type=MESH)

    near = sum(e.astype(jnp.int32) for _, _, e in dirs)
    lane = iota((1, 128), 1)
    zero_tile = jnp.zeros((8, 128), jnp.float32)
    edge_row = (TOP, TOP + R - 1)
    ghost_row = (TOP - 1, TOP + R)

    for d, (_, _, exists) in enumerate(dirs):
        @pl.when(jnp.logical_not(exists))
        def _():
            for f in range(1, 5):
                if d < 2:
                    press[f - 1][:, d * (D + 1), own] = jnp.zeros((2, R, H), jnp.float32)
                elif d < 4:
                    row = pl.ds(ghost_row[d - 2], 1)
                    press[f - 1][:, planes, row] = jnp.zeros((2, D, 1, H), jnp.float32)
                else:
                    xrecv[f, d - 4] = zero_tile
            if d >= 4:
                for place in (xw, xf):
                    place[d - 4] = jnp.zeros(place.shape[1:], jnp.float32)
            elif d >= 2:
                for place in (yw, yf):
                    place[d - 2] = jnp.zeros(place.shape[1:], jnp.float32)
    far = {}
    for dz in range(-REACH, REACH + 1):
        if dz:
            far[dz] = jnp.logical_and(ix + dz >= 0, ix + dz < nx)

            @pl.when(jnp.logical_not(far[dz]))
            def _():
                for place in (zw, zf):
                    place[dz + REACH] = jnp.zeros(place.shape[1:], jnp.float32)

    acc[...] = jnp.zeros(acc.shape, jnp.float32)

    def fine_copy(f, d, incoming=False):
        axis, other, _ = dirs[d]
        end = d ^ 1
        field = kx if f == KF else press[f - 1]
        if d < 2:
            here = field.at[:, 1 if d == 0 else D, own]
            there = field.at[:, D + 1 if d == 0 else 0, own]
            back = field.at[:, 0 if d == 0 else D + 1, own]
        elif d < 4:
            here = field.at[:, planes, pl.ds(edge_row[d - 2], 1)]
            there = field.at[:, planes, pl.ds(ghost_row[end - 2], 1)]
            back = field.at[:, planes, pl.ds(ghost_row[d - 2], 1)]
        else:
            here, there, back = xsend.at[f, d - 4], xrecv.at[f, end - 4], xrecv.at[f, d - 4]
        return pltpu.make_async_remote_copy(
            src_ref=here,
            dst_ref=back if incoming else there,
            send_sem=fsend.at[f, d],
            recv_sem=frecv.at[f, d if incoming else end],
            device_id={axis: other},
            device_id_type=MESH,
        )

    groups = ((own_w, xw, zw, yw), (own_f, xf, zf, yf))

    def coarse_copy(q, stage, way, incoming=False):
        own_q, x_q, z_q, y_q = groups[q]
        if stage == "z":
            here, place = z_q.at[REACH], z_q
            slot = REACH + way if incoming else REACH - way
            sems, to = (czs, czr), {"gx": ix + way}
            sent = REACH + way
        else:
            axis, other, _ = dirs[(4 if stage == "x" else 2) + way]
            here, place = (own_q, x_q) if stage == "x" else (z_q.at[pl.ds(1, BLOCKS - 2)], y_q)
            slot = way if incoming else 1 - way
            sems, to = (cxs, cxr) if stage == "x" else (cys, cyr), {axis: other}
            sent = way
        return pltpu.make_async_remote_copy(
            src_ref=here, dst_ref=place.at[slot], send_sem=sems[0].at[q, sent],
            recv_sem=sems[1].at[q, slot], device_id=to, device_id_type=MESH,
        )

    def ways(stage):
        if stage == "z":
            return list(far.items())
        first = 4 if stage == "x" else 2
        return [(way, dirs[first + way][2]) for way in range(2)]

    def coarse_start(q, stage):
        for way, exists in ways(stage):
            @pl.when(exists)
            def _():
                coarse_copy(q, stage, way).start()

    def coarse_arrive(q, stage):
        for way, exists in ways(stage):
            @pl.when(exists)
            def _():
                coarse_copy(q, stage, way, True).wait_recv()

    def coarse_sent(q, stage):
        for way, exists in ways(stage):
            @pl.when(exists)
            def _():
                coarse_copy(q, stage, way).wait_send()

    def start(make, f, which):
        for d in which:
            @pl.when(dirs[d][2])
            def _():
                make(f, d).start()

    def arrive(make, f, which):
        for d in which:
            @pl.when(dirs[d][2])
            def _():
                make(f, d, True).wait_recv()

    def edges_of(columns, offsets):
        low, high = zero_tile, zero_tile
        for j, at in enumerate(offsets):
            for t in range(T):
                to = 16 * t + at
                left = columns(j, 0, t)
                low = jnp.where(lane == to, pltpu.roll(left, to, 1) if to else left, low)
                right = columns(j, 1, t)
                high = jnp.where(lane == to, pltpu.roll(right, (to + 1) % 128, 1), high)
        return low, high

    def keep_packed(f, faces):
        xsend[f, 0] = faces[0]
        xsend[f, 1] = faces[1]

    def ghosts(f, base, offsets):
        low = pltpu.roll(xrecv[f, 0], lax.rem(128 - base, 128), 1)
        high = pltpu.roll(xrecv[f, 1], lax.rem(128 - base, 128), 1)
        lows, highs = [], []
        for at in offsets:
            lows.append([pltpu.roll(low, (128 - 16 * t - at) % 128, 1) for t in range(T)])
            highs.append([pltpu.roll(high, (255 - 16 * t - at) % 128, 1) for t in range(T)])
        return lows, highs

    def around(field, z, g, low_ghosts, high_ghosts):
        n = GROUP // 8
        lows = jnp.concatenate(low_ghosts[g * n : g * n + n], 0)
        highs = jnp.concatenate(high_ghosts[g * n : g * n + n], 0)
        at = TOP + g * GROUP
        own_rows = [field[h, z + 1, pl.ds(at, GROUP), :] for h in range(2)]
        low_y = [field[h, z + 1, pl.ds(at - 1, GROUP), :] for h in range(2)]
        high_y = [field[h, z + 1, pl.ds(at + 1, GROUP), :] for h in range(2)]
        rl, rr = [pltpu.roll(v, 1, 1) for v in own_rows]
        low_x = [jnp.where(lane == 0, lows, rl), jnp.where(lane == 0, rl, rr)]
        sl, sr = [pltpu.roll(v, H - 1, 1) for v in own_rows]
        high_x = [jnp.where(lane == H - 1, sr, sl), jnp.where(lane == H - 1, highs, sr)]
        return own_rows, low_y, high_y, low_x, high_x

    loads[0].wait()
    loads[1].wait()
    loads[2].wait()
    loads[3].wait()

    def pack(i, faces):
        z = 4 * i
        mine = lax.rem(lane, 16) // 4 == i
        result = []
        for n, field in enumerate((kx, p0)):
            fresh = edges_of(
                lambda j, h, t: field[h, z + 1 + j, pl.ds(TOP + 8 * t, 8), :], range(4)
            )
            for m in range(2):
                moved = pltpu.roll(fresh[m], z, 1)
                result.append(jnp.where(mine, moved, faces[2 * n + m]))
        return tuple(result)

    packed = lax.fori_loop(0, D // 4, pack, (zero_tile,) * 4)
    keep_packed(KF, packed[:2])
    keep_packed(1, packed[2:])

    for d, (_, _, exists) in enumerate(dirs):
        @pl.when(jnp.logical_not(exists))
        def _():
            if d < 2:
                kx[:, d * (D + 1), own] = kx[:, 1 + d * (D - 1), own]
            elif d < 4:
                kx[:, planes, pl.ds(ghost_row[d - 2], 1)] = kx[:, planes, pl.ds(edge_row[d - 2], 1)]
            else:
                xrecv[KF, d - 4] = xsend[KF, d - 4]

    pl.semaphore_wait(barrier, near + (plane_group - 1) + (nx - 1))
    start(fine_copy, KF, (4, 5, 2, 3, 0, 1))
    start(fine_copy, 1, (4, 5, 2, 3, 0, 1))

    column, spot = iota((W, 128), 0), iota((W, 128), 1)
    home = spot == FIRST + column // RATIO
    gsum[...] = jnp.where(home, 1.0, 0.0).astype(jnp.bfloat16)
    gpick[...] = jnp.where(
        jnp.logical_and(home, lax.rem(column, RATIO) == 0), 1.0, 0.0
    ).astype(jnp.bfloat16)

    arrive(fine_copy, KF, range(6))

    def weigh(i, carry):
        zs = (2 * i, 2 * i + 1)
        lows, highs = ghosts(KF, zs[0], (0, 1))
        for j, z in enumerate(zs):
            for g in range(R // GROUP):
                rows = pl.ds(g * GROUP, GROUP)
                k, *others = around(kx, z, g, lows[j], highs[j])
                for h in range(2):
                    at = pl.ds(TOP + g * GROUP, GROUP)
                    half = 0.5 * k[h]
                    low_z = half + 0.5 * kx[h, z, at, :]
                    high_z = half + 0.5 * kx[h, z + 2, at, :]
                    total = low_z + high_z
                    wz[h, z, rows, :] = low_z
                    for ref, other in zip((wyl, wyh, wxl, wxh), others):
                        face = half + 0.5 * other[h]
                        ref[h, z, rows, :] = face
                        total = total + face
                    dia[h, z, rows, :] = total
                    dinv[h, z, rows, :] = OMEGA / total
        return carry

    lax.fori_loop(0, D // 2, weigh, 0)
    for h in range(2):
        wz[h, D] = 0.5 * (kx[h, D, own, :] + kx[h, D + 1, own, :])

    def tile_sum(plane):
        return jnp.sum(plane.reshape(T, RATIO, H), axis=1)

    def wide(parts):
        return jnp.concatenate(parts, axis=1)

    def halves(make):
        return wide([make(0), make(1)])

    def sum_planes(c, load):
        total = load(RATIO * c)
        for z in range(RATIO * c + 1, RATIO * c + RATIO):
            total = total + load(z)
        return total

    def every(ref, h, c, first):
        return sum_planes(c, lambda z: ref[h, z, pl.ds(first, T, stride=RATIO), :])

    summed, picked, last = [], [], []
    for c in range(2):
        summed += [
            halves(lambda h: tile_sum(wz[h, RATIO * c])),
            halves(lambda h: tile_sum(wz[h, RATIO * c + RATIO])),
            halves(lambda h: every(wyl, h, c, 0)),
            halves(lambda h: every(wyh, h, c, RATIO - 1)),
        ]
        picked.append(halves(lambda h: tile_sum(sum_planes(c, lambda z: wxl[h, z]))))
        last.append(tile_sum(sum_planes(c, lambda z: wxh[1, z])))
    sums = select_dot(jnp.concatenate(summed, 0), gsum[...], 0)
    picks = select_dot(jnp.concatenate(picked, 0), gpick[...], 0)

    def pair(low, high):
        return low + pltpu.roll(high, SLOT, 1)

    zl, zh, yl, yh = [pair(sums[8 * n : 8 * n + 8], sums[8 * n + 32 : 8 * n + 40]) for n in range(4)]
    xl = pair(picks[:8], picks[8:])
    inside = lax.rem(lane, SLOT)
    final_lane = FIRST + CX - 1
    xh = pltpu.roll(xl, 127, 1)
    for c in range(2):
        to = c * SLOT + final_lane
        xh = jnp.where(lane == to, pltpu.roll(last[c], (to + 1) % 128, 1), xh)
    valid = jnp.logical_and(inside >= FIRST, inside <= final_lane)
    xh = jnp.where(valid, xh, 0.0)
    cdiag = zl + zh + yl + yh + xl + xh
    scale = jnp.where(valid, OMEGA / jnp.where(valid, cdiag, 1.0), 0.0)
    weights = (zl, zh, yl, yh, xl, xh)
    for n, field in enumerate((zl, yl, xl, scale)):
        own_w[n] = field
    coarse_start(0, "x")
    tile_row = iota((8, 1), 0)
    even = lane < SLOT
    edges = (
        even, jnp.logical_not(even), tile_row == 0, tile_row == 7,
        inside == FIRST, inside == final_lane,
    )
    outside = zero_tile
    for (_, _, exists), edge, w in zip(dirs, edges, weights):
        gone = jnp.where(exists, 0.0, 1.0)
        outside = outside + jnp.where(edge, gone * w, 0.0)
    diag_sum = jnp.sum(cdiag, keepdims=True)

    loads[4].wait()
    loads[5].wait()

    def sweep_planes(n, base, offsets, faces, placed=None):
        field = press[n - 1]
        lows, highs = ghosts(n, base, offsets)
        tiles = {}
        for j, at_z in enumerate(offsets):
            z = base + at_z
            for g in range(R // GROUP):
                rows = pl.ds(g * GROUP, GROUP)
                v, *others = around(field, z, g, lows[j], highs[j])
                for h in range(2):
                    at = pl.ds(TOP + g * GROUP, GROUP)
                    flux = src[h, z, rows, :] + wz[h, z, rows, :] * field[h, z, at, :]
                    flux = flux + wz[h, z + 1, rows, :] * field[h, z + 2, at, :]
                    for ref, other in zip((wyl, wyh, wxl, wxh), others):
                        flux = flux + ref[h, z, rows, :] * other[h]
                    if n == 1:
                        acc[h, z // RATIO, rows, :] += flux - dia[h, z, rows, :] * v[h]
                    new = (1.0 - OMEGA) * v[h] + dinv[h, z, rows, :] * flux
                    if n < SWEEPS:
                        press[n][h, z + 1, at, :] = new
                        for t in range(GROUP // 8):
                            tiles[j, h, g * (GROUP // 8) + t] = new[8 * t : 8 * t + 8]
                    else:
                        out[z, rows, pl.ds(h * H, H)] = new + corr[z // RATIO, h, rows, :]
        if n == SWEEPS:
            return faces
        fresh = edges_of(lambda j, h, t: tiles[j, h, t], offsets)
        if placed is None:
            return fresh
        place = lax.rem(lane, 16)
        mine = jnp.logical_and(place >= base + offsets[0], place <= base + offsets[-1])
        return tuple(jnp.where(mine, pltpu.roll(a, base, 1), b) for a, b in zip(fresh, faces))

    def sweep(n):
        arrive(fine_copy, n, range(6))
        if n == SWEEPS:
            lax.fori_loop(0, D // 2, lambda i, c: sweep_planes(n, 2 * i, (0, 1), c, True), 0)
            return
        faces = sweep_planes(n, 0, (0, D - 1), None)

        def inner(i, faces):
            return sweep_planes(n, 2 * i + 1, (0, 1), faces, True)

        faces = lax.fori_loop(0, 1, inner, faces)
        start(fine_copy, n + 1, (0, 1))
        faces = lax.fori_loop(1, D // 2 - 1, inner, faces)
        keep_packed(n + 1, faces)
        start(fine_copy, n + 1, (4, 5, 2, 3))

    sweep(1)

    resid = select_dot(
        jnp.concatenate([halves(lambda h: tile_sum(acc[h, c])) for c in range(2)], 0), gsum[...], 0
    )
    rhs = pair(resid[:8], resid[8:])
    fixed = scale * rhs

    own_f[0] = fixed
    coarse_start(1, "x")

    def merge(q):
        own_q, x_q, z_q, _ = groups[q]
        for n in range(own_q.shape[0]):
            low, high = pltpu.roll(x_q[0, n], 128 - CX, 1), pltpu.roll(x_q[1, n], CX, 1)
            after = jnp.logical_and(inside > final_lane, inside <= final_lane + RATIO)
            z_q[REACH, n] = jnp.where(inside < FIRST, low, jnp.where(after, high, own_q[n]))

    for stage, later in (("x", "z"), ("z", "y")):
        for q in range(2):
            coarse_arrive(q, stage)
            if stage == "x":
                merge(q)
            coarse_start(q, later)

    sweep(2)

    def extended(q, b, n):
        _, _, z_q, y_q = groups[q]
        if b in (0, BLOCKS - 1):
            return jnp.concatenate([zero_tile, z_q[b, n], zero_tile], 0)
        return jnp.concatenate([y_q[0, b - 1, n], z_q[b, n], y_q[1, b - 1, n]], 0)

    def other_slot(v):
        return pltpu.roll(v, SLOT, 1)

    coarse_arrive(0, "y")
    turned = [other_slot(extended(0, b, 0)) for b in range(BLOCKS)]
    tall = 3 * RATIO
    for b in range(1, BLOCKS - 1):
        wz_b, wy_b, wx_b, scale_b = [extended(0, b, n) for n in range(4)]
        high = (
            jnp.where(even, turned[b], turned[b + 1]),
            pltpu.roll(wy_b, tall - 1, 0),
            pltpu.roll(wx_b, 127, 1),
        )
        for n, w in enumerate((wz_b, high[0], wy_b, high[1], wx_b, high[2])):
            sides[b - 1, n] = scale_b * w

    coarse_arrive(1, "y")
    start_values = [extended(1, b, 0) for b in range(BLOCKS)]
    e = list(start_values)
    for m in range(1, COARSE_SWEEPS):
        turned = [other_slot(v) for v in e]
        following = list(e)
        for b in range(1, BLOCKS - 1):
            if 2 * abs(b - REACH) - 1 > COARSE_SWEEPS - 1 - m:
                continue
            beside = (
                jnp.where(even, turned[b - 1], turned[b]),
                jnp.where(even, turned[b], turned[b + 1]),
                pltpu.roll(e[b], 1, 0),
                pltpu.roll(e[b], tall - 1, 0),
                pltpu.roll(e[b], 1, 1),
                pltpu.roll(e[b], 127, 1),
            )
            new = (1.0 - OMEGA) * e[b] + start_values[b]
            for n, g in enumerate(beside):
                new = new + sides[b - 1, n] * g
            following[b] = new
        e = following
    swept = e[REACH][RATIO : 2 * RATIO]

    def share(buf, ssem, rsem, count, me, peer_of):
        def copy(step, incoming):
            peer, other = peer_of(step)
            return pltpu.make_async_remote_copy(
                src_ref=buf.at[me], dst_ref=buf.at[other if incoming else me],
                send_sem=ssem.at[other], recv_sem=rsem.at[other if incoming else me],
                device_id=peer, device_id_type=MESH,
            )

        @pl.loop(1, count)
        def _(step):
            copy(step, False).start()

        def finish():
            @pl.loop(1, count)
            def _(step):
                copy(step, True).wait_recv()
            return jnp.sum(buf[...], axis=0)

        def drain():
            @pl.loop(1, count)
            def _(step):
                copy(step, False).wait_send()

        return finish, drain

    mine = jnp.sum(rhs - outside * swept, keepdims=True)
    part1[my_plane] = jnp.where(lane == 0, mine, jnp.where(lane == 1, diag_sum, 0.0))
    finish1, drain1 = share(part1, a1send, a1recv, plane_group, my_plane, plane_peer)

    both = jnp.concatenate([swept, pltpu.roll(swept, SLOT, 1)], 0)
    spread = select_dot(both, gsum[...], 1)
    for c in range(2):
        for h in range(2):
            values = spread[8 * c : 8 * c + 8, h * H : h * H + H]
            corr[c, h] = jnp.broadcast_to(values[:, None, :], (T, RATIO, H)).reshape(R, H)

    sweep(3)
    part2[ix] = finish1()
    finish2, drain2 = share(part2, a2send, a2recv, nx, ix, line_peer)

    sweep(SWEEPS)

    for f in range(5):
        for d in range(6):
            @pl.when(dirs[d][2])
            def _():
                fine_copy(f, d).wait_send()
    for q in range(2):
        for stage in ("x", "z", "y"):
            coarse_sent(q, stage)
    drain1()

    sums = finish2()
    drain2()
    top = jnp.sum(jnp.where(lane == 0, sums, 0.0), keepdims=True)
    bottom = jnp.sum(jnp.where(lane == 1, sums, 0.0), keepdims=True)
    shift_out[...] = jnp.broadcast_to(top / bottom, (8, 128))


def solution(mesh):
    nx, ny, nz = mesh.shape["gx"], mesh.shape["gy"], mesh.shape["gz"]
    f32, bf16 = jnp.float32, jnp.bfloat16
    dma = pltpu.SemaphoreType.DMA

    def body(*refs):
        kernel(nx, ny, nz, *refs)

    def shards(pressure_start, source, permeability):
        block = pltpu.VMEM((2, D, R, H), f32)
        ghosted = pltpu.VMEM((2, D + 2, R + 2 * TOP, H), f32)
        smoothed, shift = pl.pallas_call(
            body,
            out_shape=(
                jax.ShapeDtypeStruct((D, R, W), f32), jax.ShapeDtypeStruct((8, 128), f32)
            ),
            in_specs=[pl.BlockSpec(memory_space=pltpu.HBM)] * 3,
            out_specs=(
                pl.BlockSpec(memory_space=pltpu.VMEM), pl.BlockSpec(memory_space=pltpu.VMEM)
            ),
            scratch_shapes=[
                ghosted, ghosted, ghosted, ghosted, ghosted,
                block, pltpu.VMEM((2, D + 1, R, H), f32), block, block, block, block, block, block,
                pltpu.VMEM((2, 2, R, H), f32),
                pltpu.VMEM((W, 128), bf16), pltpu.VMEM((W, 128), bf16),
                pltpu.VMEM((2, 2, R, H), f32),
                pltpu.VMEM((5, 2, 8, 128), f32), pltpu.VMEM((5, 2, 8, 128), f32),
                *[
                    pltpu.VMEM(lead + (count, 8, 128), f32)
                    for count in (4, 1)
                    for lead in ((), (2,), (BLOCKS,), (2, BLOCKS - 2))
                ],
                pltpu.VMEM((BLOCKS - 2, 6, 3 * RATIO, 128), f32),
                pltpu.VMEM((ny * nz, 1, 128), f32), pltpu.VMEM((nx, 1, 128), f32),
                dma((3, 2)), dma((5, 6)), dma((5, 6)),
                dma((2, 2)), dma((2, 2)), dma((2, BLOCKS)), dma((2, BLOCKS)), dma((2, 2)), dma((2, 2)),
                dma((ny * nz,)), dma((ny * nz,)), dma((nx,)), dma((nx,)),
            ],
            compiler_params=pltpu.CompilerParams(
                collective_id=0, has_side_effects=True, vmem_limit_bytes=62 << 20
            ),
        )(pressure_start, source, permeability)
        return smoothed + shift[0, 0]

    spec = P("gx", "gy", "gz")
    return jax.shard_map(
        shards, mesh=mesh, in_specs=(spec, spec, spec), out_specs=spec, check_vma=False
    )
```

time: 73.1 us -> 48.9 us (0.67); the launches traced: 72 us -> 48.7 us
  Pallas kernels: 67.3 us -> 44.6 us
  local copies, waits for them, and re-layouts: 4.65 us -> 1.22 us
  other arithmetic: 0 us -> 2.91 us
    pallas_call x1, Pallas kernels: 67.3 us -> 44.6 us  [shards(): pl.pallas_call(body, out_shape=(jax.ShapeDtypeStruct((D, R, W), f32), jax...]
    unnamed x7 -> x0, local copies, waits for them, and re-layouts: 4.65 us -> none
    add x0 -> x1, other arithmetic: none -> 2.91 us  [shards(): return smoothed + shift[0, 0]]
    slice x0 -> x1, local copies, waits for them, and re-layouts: none -> 1.22 us  [shards(): return smoothed + shift[0, 0]]
where the time goes in v2:
time: 48.9 us; the launch traced here: 48.7 us
  Pallas kernels  44.6 us (91%)
  other arithmetic  2.91 us (6%)
  local copies, waits for them, and re-layouts  1.22 us (2%)
    pallas_call x1, Pallas kernels, shards(): pl.pallas_call(body, out_shape=(jax.ShapeDtypeStruct((D, R, W), f32), jax...  44.6 us
    add x1, other arithmetic, shards(): return smoothed + shift[0, 0]  2.91 us
    slice x1, local copies, waits for them, and re-layouts, shards(): return smoothed + shift[0, 0]  1.22 us

profile of v2, /device:TPU:1, one launch (start us, length us, event | category | flops | bytes accessed | tf_op | source)
XLA Modules:
  0.0 48.7 jit_solution(11841891276639837611)
XLA Ops:
  0.0 44.6 %shard_map.37 = (f32[16,64,256]{2,1,0:T(8,128)}, f32[8,128]{1,0:T(8,128)}) custom-call(f32[16,64,256]{2,1,0:T(8,128)} %refs_0_.1, f32[16,64,256]{2,1,0:T(8,128)} %refs_1_.1, f32[16,64,256]{2,1,0:T(8,128)} %refs_2_.1), custom_call_target="tpu_custom_call" | custom-call | tf_op jit(solution)/shard_map/pallas_call | solution.py:580
  44.6 1.2 %slice.3 = f32[1,1]{1,0:T(1,128)} slice(f32[8,128]{1,0:T(8,128)} %get-tuple-element.8), slice={[0:1], [0:1]} | slice | bytes 8 | tf_op jit(solution)/shard_map/slice | solution.py:611
  45.8 2.9 %broadcast_add_fusion = f32[16,64,256]{2,1,0:T(8,128)} fusion(f32[16,64,256]{2,1,0:T(8,128)} %get-tuple-element.7, f32[]{:T(128)} %bitcast), kind=kLoop, calls=%fused_computation | loop fusion | flops 262144 | bytes 2097156 | tf_op jit(solution)/shard_map/add | solution.py:611

commit v3 on v2

--- a/solution.py
+++ b/solution.py
@@ -1,3 +1,5 @@
+import functools
+
 import jax
 import jax.numpy as jnp
 from jax import lax
@@ -46,7 +48,7 @@
 
 def kernel(
     nx, ny, nz,
-    p_hbm, s_hbm, k_hbm, out, shift_out,
+    p_hbm, s_hbm, k_hbm, out,
     kx, p0, p1, p2, p3, src, wz, wyl, wyh, wxl, wxh, dia, dinv, acc, gsum, gpick, corr,
     xsend, xrecv, own_w, xw, zw, yw, own_f, xf, zf, yf, sides, part1, part2,
     load_sem, fsend, frecv, cxs, cxr, czs, czr, cys, cyr, a1send, a1recv, a2send, a2recv,
@@ -210,34 +212,41 @@
             def _():
                 make(f, d, True).wait_recv()
 
-    def edges_of(columns, offsets):
-        low, high = zero_tile, zero_tile
-        for j, at in enumerate(offsets):
-            for t in range(T):
-                to = 16 * t + at
-                left = columns(j, 0, t)
-                low = jnp.where(lane == to, pltpu.roll(left, to, 1) if to else left, low)
-                right = columns(j, 1, t)
-                high = jnp.where(lane == to, pltpu.roll(right, (to + 1) % 128, 1), high)
+    def edges_of(news, g, at_z, low, high):
+        n = GROUP // 8
+        for t in range(g * n, g * n + n):
+            to = 16 * t + at_z
+            part = slice(8 * (t - g * n), 8 * (t - g * n) + 8)
+            left, right = news[0][part], news[1][part]
+            low = jnp.where(lane == to, pltpu.roll(left, to, 1) if to else left, low)
+            high = jnp.where(
+                lane == to, pltpu.roll(right, to + 1, 1) if to < 127 else right, high
+            )
         return low, high
 
     def keep_packed(f, faces):
         xsend[f, 0] = faces[0]
         xsend[f, 1] = faces[1]
 
-    def ghosts(f, base, offsets):
-        low = pltpu.roll(xrecv[f, 0], lax.rem(128 - base, 128), 1)
-        high = pltpu.roll(xrecv[f, 1], lax.rem(128 - base, 128), 1)
-        lows, highs = [], []
-        for at in offsets:
-            lows.append([pltpu.roll(low, (128 - 16 * t - at) % 128, 1) for t in range(T)])
-            highs.append([pltpu.roll(high, (255 - 16 * t - at) % 128, 1) for t in range(T)])
-        return lows, highs
-
-    def around(field, z, g, low_ghosts, high_ghosts):
+    def ghosts(f, base):
+        back = lax.rem(128 - base, 128) if not isinstance(base, int) else (128 - base) % 128
+        low, high = xrecv[f, 0], xrecv[f, 1]
+        if not isinstance(base, int) or base:
+            low, high = pltpu.roll(low, back, 1), pltpu.roll(high, back, 1)
+
+        def turn(v, by):
+            return pltpu.roll(v, by % 128, 1) if by % 128 else v
+
+        return (
+            lambda at, t: turn(low, 128 - 16 * t - at),
+            lambda at, t: turn(high, 255 - 16 * t - at),
+        )
+
+    def around(field, z, g, at_z, makers):
         n = GROUP // 8
-        lows = jnp.concatenate(low_ghosts[g * n : g * n + n], 0)
-        highs = jnp.concatenate(high_ghosts[g * n : g * n + n], 0)
+        lows, highs = [
+            jnp.concatenate([make(at_z, t) for t in range(g * n, g * n + n)], 0) for make in makers
+        ]
         at = TOP + g * GROUP
         own_rows = [field[h, z + 1, pl.ds(at, GROUP), :] for h in range(2)]
         low_y = [field[h, z + 1, pl.ds(at - 1, GROUP), :] for h in range(2)]
@@ -248,27 +257,29 @@
         high_x = [jnp.where(lane == H - 1, sr, sl), jnp.where(lane == H - 1, highs, sr)]
         return own_rows, low_y, high_y, low_x, high_x
 
-    loads[0].wait()
-    loads[1].wait()
-    loads[2].wait()
-    loads[3].wait()
-
-    def pack(i, faces):
-        z = 4 * i
-        mine = lax.rem(lane, 16) // 4 == i
-        result = []
-        for n, field in enumerate((kx, p0)):
-            fresh = edges_of(
-                lambda j, h, t: field[h, z + 1 + j, pl.ds(TOP + 8 * t, 8), :], range(4)
-            )
-            for m in range(2):
-                moved = pltpu.roll(fresh[m], z, 1)
-                result.append(jnp.where(mine, moved, faces[2 * n + m]))
-        return tuple(result)
-
-    packed = lax.fori_loop(0, D // 4, pack, (zero_tile,) * 4)
-    keep_packed(KF, packed[:2])
-    keep_packed(1, packed[2:])
+    def pack_field(field):
+        def pack(i, faces):
+            z = 4 * i
+            fresh = (zero_tile, zero_tile)
+            for j in range(4):
+                for g in range(R // GROUP):
+                    at = pl.ds(TOP + g * GROUP, GROUP)
+                    rows = [field[h, z + 1 + j, at, :] for h in range(2)]
+                    fresh = edges_of(rows, g, j, *fresh)
+            mine = lax.rem(lane, 16) // 4 == i
+            return tuple(jnp.where(mine, pltpu.roll(a, z, 1), b) for a, b in zip(fresh, faces))
+
+        return lax.fori_loop(0, D // 4, pack, (zero_tile, zero_tile))
+
+    for load in loads[:2]:
+        load.wait()
+    keep_packed(KF, pack_field(kx))
+    pl.semaphore_wait(barrier, near + (plane_group - 1) + (nx - 1))
+    start(fine_copy, KF, (4, 5, 2, 3, 0, 1))
+    for load in loads[2:4]:
+        load.wait()
+    keep_packed(1, pack_field(p0))
+    start(fine_copy, 1, (4, 5, 2, 3, 0, 1))
 
     for d, (_, _, exists) in enumerate(dirs):
         @pl.when(jnp.logical_not(exists))
@@ -280,10 +291,6 @@
             else:
                 xrecv[KF, d - 4] = xsend[KF, d - 4]
 
-    pl.semaphore_wait(barrier, near + (plane_group - 1) + (nx - 1))
-    start(fine_copy, KF, (4, 5, 2, 3, 0, 1))
-    start(fine_copy, 1, (4, 5, 2, 3, 0, 1))
-
     column, spot = iota((W, 128), 0), iota((W, 128), 1)
     home = spot == FIRST + column // RATIO
     gsum[...] = jnp.where(home, 1.0, 0.0).astype(jnp.bfloat16)
@@ -291,15 +298,15 @@
         jnp.logical_and(home, lax.rem(column, RATIO) == 0), 1.0, 0.0
     ).astype(jnp.bfloat16)
 
-    arrive(fine_copy, KF, range(6))
-
-    def weigh(i, carry):
-        zs = (2 * i, 2 * i + 1)
-        lows, highs = ghosts(KF, zs[0], (0, 1))
-        for j, z in enumerate(zs):
+    arrive(fine_copy, KF, range(2, 6))
+
+    def weigh(base, offsets):
+        makers = ghosts(KF, base)
+        for at_z in offsets:
+            z = base + at_z
             for g in range(R // GROUP):
                 rows = pl.ds(g * GROUP, GROUP)
-                k, *others = around(kx, z, g, lows[j], highs[j])
+                k, *others = around(kx, z, g, at_z, makers)
                 for h in range(2):
                     at = pl.ds(TOP + g * GROUP, GROUP)
                     half = 0.5 * k[h]
@@ -313,9 +320,13 @@
                         total = total + face
                     dia[h, z, rows, :] = total
                     dinv[h, z, rows, :] = OMEGA / total
-        return carry
-
-    lax.fori_loop(0, D // 2, weigh, 0)
+
+    @pl.loop(0, D // 2 - 1)
+    def _(i):
+        weigh(2 * i + 1, (0, 1))
+
+    arrive(fine_copy, KF, (0, 1))
+    weigh(0, (0, D - 1))
     for h in range(2):
         wz[h, D] = 0.5 * (kx[h, D, own, :] + kx[h, D + 1, own, :])
 
@@ -381,18 +392,32 @@
         outside = outside + jnp.where(edge, gone * w, 0.0)
     diag_sum = jnp.sum(cdiag, keepdims=True)
 
+    def merge(q):
+        own_q, x_q, z_q, _ = groups[q]
+        for n in range(own_q.shape[0]):
+            low, high = pltpu.roll(x_q[0, n], 128 - CX, 1), pltpu.roll(x_q[1, n], CX, 1)
+            after = jnp.logical_and(inside > final_lane, inside <= final_lane + RATIO)
+            z_q[REACH, n] = jnp.where(inside < FIRST, low, jnp.where(after, high, own_q[n]))
+
+    def push_weights():
+        coarse_arrive(0, "x")
+        merge(0)
+        coarse_start(0, "z")
+
     loads[4].wait()
     loads[5].wait()
 
-    def sweep_planes(n, base, offsets, faces, placed=None):
+    def sweep_planes(n, base, offsets, faces):
         field = press[n - 1]
-        lows, highs = ghosts(n, base, offsets)
-        tiles = {}
-        for j, at_z in enumerate(offsets):
+        makers = ghosts(n, base)
+        low, high = zero_tile, zero_tile
+        fresh = []
+        for at_z in offsets:
             z = base + at_z
             for g in range(R // GROUP):
                 rows = pl.ds(g * GROUP, GROUP)
-                v, *others = around(field, z, g, lows[j], highs[j])
+                v, *others = around(field, z, g, at_z, makers)
+                news = []
                 for h in range(2):
                     at = pl.ds(TOP + g * GROUP, GROUP)
                     flux = src[h, z, rows, :] + wz[h, z, rows, :] * field[h, z, at, :]
@@ -404,34 +429,46 @@
                     new = (1.0 - OMEGA) * v[h] + dinv[h, z, rows, :] * flux
                     if n < SWEEPS:
                         press[n][h, z + 1, at, :] = new
-                        for t in range(GROUP // 8):
-                            tiles[j, h, g * (GROUP // 8) + t] = new[8 * t : 8 * t + 8]
+                        news.append(new)
                     else:
                         out[z, rows, pl.ds(h * H, H)] = new + corr[z // RATIO, h, rows, :]
+                if n < SWEEPS:
+                    fresh.append((news, g, at_z))
         if n == SWEEPS:
             return faces
-        fresh = edges_of(lambda j, h, t: tiles[j, h, t], offsets)
-        if placed is None:
-            return fresh
+        for news, g, at_z in fresh:
+            low, high = edges_of(news, g, at_z, low, high)
         place = lax.rem(lane, 16)
-        mine = jnp.logical_and(place >= base + offsets[0], place <= base + offsets[-1])
-        return tuple(jnp.where(mine, pltpu.roll(a, base, 1), b) for a, b in zip(fresh, faces))
+        if isinstance(base, int):
+            mine = functools.reduce(jnp.logical_or, [place == base + at_z for at_z in offsets])
+        else:
+            low, high = pltpu.roll(low, base, 1), pltpu.roll(high, base, 1)
+            mine = jnp.logical_and(place >= base + offsets[0], place <= base + offsets[-1])
+        return jnp.where(mine, low, faces[0]), jnp.where(mine, high, faces[1])
+
+    none = (zero_tile, zero_tile)
+    rim = (0, D - 1)
 
     def sweep(n):
+        def inner(i, faces):
+            return sweep_planes(n, 2 * i + 1, (0, 1), faces)
+
+        count = D // 2 - 1
+        if n == 1:
+            arrive(fine_copy, n, range(2, 6))
+            faces = lax.fori_loop(0, count, inner, none)
+            arrive(fine_copy, n, (0, 1))
+            keep_packed(n + 1, sweep_planes(n, 0, rim, faces))
+            return
         arrive(fine_copy, n, range(6))
-        if n == SWEEPS:
-            lax.fori_loop(0, D // 2, lambda i, c: sweep_planes(n, 2 * i, (0, 1), c, True), 0)
-            return
-        faces = sweep_planes(n, 0, (0, D - 1), None)
-
-        def inner(i, faces):
-            return sweep_planes(n, 2 * i + 1, (0, 1), faces, True)
-
-        faces = lax.fori_loop(0, 1, inner, faces)
-        start(fine_copy, n + 1, (0, 1))
-        faces = lax.fori_loop(1, D // 2 - 1, inner, faces)
-        keep_packed(n + 1, faces)
-        start(fine_copy, n + 1, (4, 5, 2, 3))
+        faces = sweep_planes(n, 0, rim, none)
+        if n < SWEEPS:
+            faces = lax.fori_loop(0, 1, inner, faces)
+            start(fine_copy, n + 1, (0, 1))
+        faces = lax.fori_loop(1 if n < SWEEPS else 0, count, inner, faces)
+        if n < SWEEPS:
+            keep_packed(n + 1, faces)
+            start(fine_copy, n + 1, (4, 5, 2, 3))
 
     sweep(1)
 
@@ -443,20 +480,15 @@
 
     own_f[0] = fixed
     coarse_start(1, "x")
-
-    def merge(q):
-        own_q, x_q, z_q, _ = groups[q]
-        for n in range(own_q.shape[0]):
-            low, high = pltpu.roll(x_q[0, n], 128 - CX, 1), pltpu.roll(x_q[1, n], CX, 1)
-            after = jnp.logical_and(inside > final_lane, inside <= final_lane + RATIO)
-            z_q[REACH, n] = jnp.where(inside < FIRST, low, jnp.where(after, high, own_q[n]))
-
-    for stage, later in (("x", "z"), ("z", "y")):
-        for q in range(2):
-            coarse_arrive(q, stage)
-            if stage == "x":
-                merge(q)
-            coarse_start(q, later)
+    start(fine_copy, 2, (4, 5, 2, 3, 0, 1))
+    push_weights()
+
+    coarse_arrive(1, "x")
+    merge(1)
+    coarse_start(1, "z")
+    for q in range(2):
+        coarse_arrive(q, "z")
+        coarse_start(q, "y")
 
     sweep(2)
 
@@ -563,7 +595,12 @@
     drain2()
     top = jnp.sum(jnp.where(lane == 0, sums, 0.0), keepdims=True)
     bottom = jnp.sum(jnp.where(lane == 1, sums, 0.0), keepdims=True)
-    shift_out[...] = jnp.broadcast_to(top / bottom, (8, 128))
+    shift = top / bottom
+
+    @pl.loop(0, D // 4)
+    def _(i):
+        for j in range(4):
+            out[4 * i + j] = out[4 * i + j] + shift
 
 
 def solution(mesh):
@@ -574,18 +611,14 @@
     def body(*refs):
         kernel(nx, ny, nz, *refs)
 
-    def shards(pressure_start, source, permeability):
+    def shards(*arrays):
         block = pltpu.VMEM((2, D, R, H), f32)
         ghosted = pltpu.VMEM((2, D + 2, R + 2 * TOP, H), f32)
-        smoothed, shift = pl.pallas_call(
+        return pl.pallas_call(
             body,
-            out_shape=(
-                jax.ShapeDtypeStruct((D, R, W), f32), jax.ShapeDtypeStruct((8, 128), f32)
-            ),
+            out_shape=jax.ShapeDtypeStruct((D, R, W), f32),
             in_specs=[pl.BlockSpec(memory_space=pltpu.HBM)] * 3,
-            out_specs=(
-                pl.BlockSpec(memory_space=pltpu.VMEM), pl.BlockSpec(memory_space=pltpu.VMEM)
-            ),
+            out_specs=pl.BlockSpec(memory_space=pltpu.VMEM),
             scratch_shapes=[
                 ghosted, ghosted, ghosted, ghosted, ghosted,
                 block, pltpu.VMEM((2, D + 1, R, H), f32), block, block, block, block, block, block,
@@ -605,10 +638,9 @@
                 dma((ny * nz,)), dma((ny * nz,)), dma((nx,)), dma((nx,)),
             ],
             compiler_params=pltpu.CompilerParams(
-                collective_id=0, has_side_effects=True, vmem_limit_bytes=62 << 20
+                collective_id=0, has_side_effects=True, vmem_limit_bytes=40 << 20
             ),
-        )(pressure_start, source, permeability)
-        return smoothed + shift[0, 0]
+        )(*[pltpu.with_memory_space_constraint(a, pltpu.HBM) for a in arrays])
 
     spec = P("gx", "gy", "gz")
     return jax.shard_map(

time: 48.9 us -> 45.4 us (0.928)
  other arithmetic: 2.91 us -> 0 us
    add x1 -> x0, other arithmetic: 2.91 us -> none  [shards(): return smoothed + shift[0, 0]]
    slice x1 -> x0, local copies, waits for them, and re-layouts: 1.22 us -> none  [shards(): return smoothed + shift[0, 0]]
    unnamed x0 -> x1, local copies, waits for them, and re-layouts: none -> 0.97 us
where the time goes in v3:
time: 45.4 us
  Pallas kernels  44.4 us (98%)
  local copies, waits for them, and re-layouts  0.97 us (2%)
    pallas_call x1, Pallas kernels, shards(): pl.pallas_call(body, out_shape=jax.ShapeDtypeStruct((D, R, W), f32), in_s...  44.4 us
    unnamed x1, local copies, waits for them, and re-layouts  0.97 us

profile of v3, /device:TPU:1, one launch (start us, length us, event | category | flops | bytes accessed | tf_op | source)
XLA Modules:
  0.0 45.4 jit_solution(17601706934433311749)
XLA Ops:
  0.0 44.4 %shard_map.37 = f32[16,64,256]{2,1,0:T(8,128)S(1)} custom-call(f32[16,64,256]{2,1,0:T(8,128)} %refs_0_.1, f32[16,64,256]{2,1,0:T(8,128)} %refs_1_.1, f32[16,64,256]{2,1,0:T(8,128)} %refs_2_.1), custom_call_target="tpu_custom_call" | custom-call | tf_op jit(solution)/shard_map/pallas_call | solution.py:617
  44.4 1.0 %copy.5 = f32[16,64,256]{2,1,0:T(8,128)} copy(f32[16,64,256]{2,1,0:T(8,128)S(1)} %shard_map.37) | data formatting | bytes 2097152

commit v4 on v3

--- a/solution.py
+++ b/solution.py
@@ -23,6 +23,7 @@
 REACH = 4
 BLOCKS = 2 * REACH + 1
 KF = 0
+CHUNK = R // 2
 GROUP = 16
 
 
@@ -77,26 +78,19 @@
 
     barrier = pltpu.get_barrier_semaphore()
 
-    def plane_peer(step):
-        other = lax.rem(my_plane + step, plane_group)
-        return {"gy": other // nz, "gz": lax.rem(other, nz)}, other
-
-    def line_peer(step):
-        other = lax.rem(ix + step, nx)
-        return {"gx": other}, other
+    plane_peers = [
+        {"gy": lax.rem(iy + dy, ny), "gz": lax.rem(iz + dz, nz)}
+        for dy in range(ny) for dz in range(nz) if dy or dz
+    ]
+    line_peers = [{"gx": lax.rem(ix + step, nx)} for step in range(1, nx)]
 
     for axis, other, exists in dirs:
         @pl.when(exists)
         def _():
             pl.semaphore_signal(barrier, 1, device_id={axis: other}, device_id_type=MESH)
 
-    @pl.loop(1, plane_group)
-    def _(step):
-        pl.semaphore_signal(barrier, 1, device_id=plane_peer(step)[0], device_id_type=MESH)
-
-    @pl.loop(1, nx)
-    def _(step):
-        pl.semaphore_signal(barrier, 1, device_id=line_peer(step)[0], device_id_type=MESH)
+    for peer in plane_peers + line_peers:
+        pl.semaphore_signal(barrier, 1, device_id=peer, device_id_type=MESH)
 
     near = sum(e.astype(jnp.int32) for _, _, e in dirs)
     lane = iota((1, 128), 1)
@@ -134,13 +128,16 @@
     acc[...] = jnp.zeros(acc.shape, jnp.float32)
 
     def fine_copy(f, d, incoming=False):
+        chunk, d = d // 6, d % 6
         axis, other, _ = dirs[d]
+        rows = pl.ds(TOP + chunk * CHUNK, CHUNK)
+        shift = 6 * chunk
         end = d ^ 1
         field = kx if f == KF else press[f - 1]
         if d < 2:
-            here = field.at[:, 1 if d == 0 else D, own]
-            there = field.at[:, D + 1 if d == 0 else 0, own]
-            back = field.at[:, 0 if d == 0 else D + 1, own]
+            here = field.at[:, 1 if d == 0 else D, rows]
+            there = field.at[:, D + 1 if d == 0 else 0, rows]
+            back = field.at[:, 0 if d == 0 else D + 1, rows]
         elif d < 4:
             here = field.at[:, planes, pl.ds(edge_row[d - 2], 1)]
             there = field.at[:, planes, pl.ds(ghost_row[end - 2], 1)]
@@ -150,8 +147,8 @@
         return pltpu.make_async_remote_copy(
             src_ref=here,
             dst_ref=back if incoming else there,
-            send_sem=fsend.at[f, d],
-            recv_sem=frecv.at[f, d if incoming else end],
+            send_sem=fsend.at[f, d + shift],
+            recv_sem=frecv.at[f, (d if incoming else end) + shift],
             device_id={axis: other},
             device_id_type=MESH,
         )
@@ -161,54 +158,69 @@
     def coarse_copy(q, stage, way, incoming=False):
         own_q, x_q, z_q, y_q = groups[q]
         if stage == "z":
-            here, place = z_q.at[REACH], z_q
             slot = REACH + way if incoming else REACH - way
+            here, there = z_q.at[REACH], z_q.at[slot]
+            if q == 0 and abs(way) == REACH:
+                here, there = here.at[pl.ds(0, 1)], there.at[pl.ds(0, 1)]
             sems, to = (czs, czr), {"gx": ix + way}
             sent = REACH + way
         else:
-            axis, other, _ = dirs[(4 if stage == "x" else 2) + way]
-            here, place = (own_q, x_q) if stage == "x" else (z_q.at[pl.ds(1, BLOCKS - 2)], y_q)
-            slot = way if incoming else 1 - way
-            sems, to = (cxs, cxr) if stage == "x" else (cys, cyr), {axis: other}
-            sent = way
+            piece, side = way // 2, way % 2
+            axis, other, _ = dirs[(4 if stage == "x" else 2) + side]
+            slot = way if incoming else way ^ 1
+            if stage == "x":
+                here, there, sems = own_q, x_q.at[slot], (cxs, cxr)
+            else:
+                first, size = ((REACH - 2, 3), (0, REACH - 2), (REACH + 1, REACH - 2))[piece]
+                here = z_q.at[pl.ds(first + 1, size)]
+                there = y_q.at[slot % 2, pl.ds(first, size)]
+                sems = (cys, cyr)
+            to, sent = {axis: other}, way
         return pltpu.make_async_remote_copy(
-            src_ref=here, dst_ref=place.at[slot], send_sem=sems[0].at[q, sent],
+            src_ref=here, dst_ref=there, send_sem=sems[0].at[q, sent],
             recv_sem=sems[1].at[q, slot], device_id=to, device_id_type=MESH,
         )
 
-    def ways(stage):
+    def ways(q, stage, incoming):
         if stage == "z":
-            return list(far.items())
+            useless = (-REACH if incoming else REACH) if q == 0 else 0
+            return [(way, exists) for way, exists in far.items() if way != useless]
         first = 4 if stage == "x" else 2
-        return [(way, dirs[first + way][2]) for way in range(2)]
-
-    def coarse_start(q, stage):
-        for way, exists in ways(stage):
+        return [(way, dirs[first + way % 2][2]) for way in range(2 if stage == "x" else 6)]
+
+    def coarse_start(q, stage, only=None):
+        for way, exists in ways(q, stage, False):
+            if only is not None and way not in only:
+                continue
+
             @pl.when(exists)
             def _():
                 coarse_copy(q, stage, way).start()
 
-    def coarse_arrive(q, stage):
-        for way, exists in ways(stage):
+    def coarse_arrive(q, stage, only=None):
+        for way, exists in ways(q, stage, True):
+            if only is not None and way not in only:
+                continue
+
             @pl.when(exists)
             def _():
                 coarse_copy(q, stage, way, True).wait_recv()
 
     def coarse_sent(q, stage):
-        for way, exists in ways(stage):
+        for way, exists in ways(q, stage, False):
             @pl.when(exists)
             def _():
                 coarse_copy(q, stage, way).wait_send()
 
     def start(make, f, which):
         for d in which:
-            @pl.when(dirs[d][2])
+            @pl.when(dirs[d % 6][2])
             def _():
                 make(f, d).start()
 
     def arrive(make, f, which):
         for d in which:
-            @pl.when(dirs[d][2])
+            @pl.when(dirs[d % 6][2])
             def _():
                 make(f, d, True).wait_recv()
 
@@ -275,11 +287,11 @@
         load.wait()
     keep_packed(KF, pack_field(kx))
     pl.semaphore_wait(barrier, near + (plane_group - 1) + (nx - 1))
-    start(fine_copy, KF, (4, 5, 2, 3, 0, 1))
+    start(fine_copy, KF, (4, 5, 2, 3, 0, 1, 6, 7))
     for load in loads[2:4]:
         load.wait()
     keep_packed(1, pack_field(p0))
-    start(fine_copy, 1, (4, 5, 2, 3, 0, 1))
+    start(fine_copy, 1, (4, 5, 2, 3, 0, 1, 6, 7))
 
     for d, (_, _, exists) in enumerate(dirs):
         @pl.when(jnp.logical_not(exists))
@@ -325,7 +337,7 @@
     def _(i):
         weigh(2 * i + 1, (0, 1))
 
-    arrive(fine_copy, KF, (0, 1))
+    arrive(fine_copy, KF, (0, 1, 6, 7))
     weigh(0, (0, D - 1))
     for h in range(2):
         wz[h, D] = 0.5 * (kx[h, D, own, :] + kx[h, D + 1, own, :])
@@ -407,14 +419,14 @@
     loads[4].wait()
     loads[5].wait()
 
-    def sweep_planes(n, base, offsets, faces):
+    def sweep_planes(n, base, offsets, faces, part=range(R // GROUP)):
         field = press[n - 1]
         makers = ghosts(n, base)
         low, high = zero_tile, zero_tile
         fresh = []
         for at_z in offsets:
             z = base + at_z
-            for g in range(R // GROUP):
+            for g in part:
                 rows = pl.ds(g * GROUP, GROUP)
                 v, *others = around(field, z, g, at_z, makers)
                 news = []
@@ -432,9 +444,9 @@
                         news.append(new)
                     else:
                         out[z, rows, pl.ds(h * H, H)] = new + corr[z // RATIO, h, rows, :]
-                if n < SWEEPS:
+                if 1 < n < SWEEPS:
                     fresh.append((news, g, at_z))
-        if n == SWEEPS:
+        if n in (1, SWEEPS):
             return faces
         for news, g, at_z in fresh:
             low, high = edges_of(news, g, at_z, low, high)
@@ -444,31 +456,38 @@
         else:
             low, high = pltpu.roll(low, base, 1), pltpu.roll(high, base, 1)
             mine = jnp.logical_and(place >= base + offsets[0], place <= base + offsets[-1])
+        tile = lane // 16
+        mine = jnp.logical_and(mine, tile >= part[0] * GROUP // 8)
+        mine = jnp.logical_and(mine, tile < (part[-1] + 1) * GROUP // 8)
         return jnp.where(mine, low, faces[0]), jnp.where(mine, high, faces[1])
 
     none = (zero_tile, zero_tile)
     rim = (0, D - 1)
 
-    def sweep(n):
+    def sweep(n, between=lambda: None):
         def inner(i, faces):
             return sweep_planes(n, 2 * i + 1, (0, 1), faces)
 
         count = D // 2 - 1
         if n == 1:
             arrive(fine_copy, n, range(2, 6))
-            faces = lax.fori_loop(0, count, inner, none)
-            arrive(fine_copy, n, (0, 1))
-            keep_packed(n + 1, sweep_planes(n, 0, rim, faces))
+            lax.fori_loop(0, count, inner, none)
+            arrive(fine_copy, n, (0, 1, 6, 7))
+            sweep_planes(n, 0, rim, none)
             return
+        first, second = range(CHUNK // GROUP), range(CHUNK // GROUP, R // GROUP)
         arrive(fine_copy, n, range(6))
-        faces = sweep_planes(n, 0, rim, none)
+        faces = sweep_planes(n, 0, rim, none, first)
         if n < SWEEPS:
             faces = lax.fori_loop(0, 1, inner, faces)
             start(fine_copy, n + 1, (0, 1))
         faces = lax.fori_loop(1 if n < SWEEPS else 0, count, inner, faces)
+        between()
+        arrive(fine_copy, n, (6, 7))
+        faces = sweep_planes(n, 0, rim, faces, second)
         if n < SWEEPS:
             keep_packed(n + 1, faces)
-            start(fine_copy, n + 1, (4, 5, 2, 3))
+            start(fine_copy, n + 1, (4, 5, 2, 3, 6, 7))
 
     sweep(1)
 
@@ -480,17 +499,23 @@
 
     own_f[0] = fixed
     coarse_start(1, "x")
-    start(fine_copy, 2, (4, 5, 2, 3, 0, 1))
+    start(fine_copy, 2, (2, 3, 0, 1))
+    keep_packed(2, pack_field(p1))
+    start(fine_copy, 2, (4, 5, 6, 7))
     push_weights()
 
     coarse_arrive(1, "x")
     merge(1)
     coarse_start(1, "z")
-    for q in range(2):
-        coarse_arrive(q, "z")
-        coarse_start(q, "y")
-
-    sweep(2)
+    def turn_to_y(q):
+        near_z = (-1, 1)
+        coarse_arrive(q, "z", near_z)
+        coarse_start(q, "y", (0, 1))
+        coarse_arrive(q, "z", [dz for dz in far if dz not in near_z])
+        coarse_start(q, "y", (2, 3, 4, 5))
+
+    turn_to_y(0)
+    sweep(2, lambda: turn_to_y(1))
 
     def extended(q, b, n):
         _, _, z_q, y_q = groups[q]
@@ -502,7 +527,7 @@
         return pltpu.roll(v, SLOT, 1)
 
     coarse_arrive(0, "y")
-    turned = [other_slot(extended(0, b, 0)) for b in range(BLOCKS)]
+    turned = [other_slot(extended(0, b, 0)) if b else None for b in range(BLOCKS)]
     tall = 3 * RATIO
     for b in range(1, BLOCKS - 1):
         wz_b, wy_b, wx_b, scale_b = [extended(0, b, n) for n in range(4)]
@@ -538,35 +563,29 @@
         e = following
     swept = e[REACH][RATIO : 2 * RATIO]
 
-    def share(buf, ssem, rsem, count, me, peer_of):
-        def copy(step, incoming):
-            peer, other = peer_of(step)
-            return pltpu.make_async_remote_copy(
-                src_ref=buf.at[me], dst_ref=buf.at[other if incoming else me],
-                send_sem=ssem.at[other], recv_sem=rsem.at[other if incoming else me],
+    def share(buf, ssem, rsem, me, peers):
+        count = len(peers) + 1
+        for peer in peers:
+            pltpu.make_async_remote_copy(
+                src_ref=buf.at[me], dst_ref=buf.at[me], send_sem=ssem.at[0], recv_sem=rsem.at[0],
                 device_id=peer, device_id_type=MESH,
-            )
-
-        @pl.loop(1, count)
-        def _(step):
-            copy(step, False).start()
+            ).start()
+
+        others = pltpu.make_async_remote_copy(
+            src_ref=buf.at[pl.ds(0, count - 1)], dst_ref=buf.at[pl.ds(0, count - 1)],
+            send_sem=ssem.at[0], recv_sem=rsem.at[0],
+            device_id=peers[0], device_id_type=MESH,
+        )
 
         def finish():
-            @pl.loop(1, count)
-            def _(step):
-                copy(step, True).wait_recv()
+            others.wait_recv()
             return jnp.sum(buf[...], axis=0)
 
-        def drain():
-            @pl.loop(1, count)
-            def _(step):
-                copy(step, False).wait_send()
-
-        return finish, drain
+        return finish, others.wait_send
 
     mine = jnp.sum(rhs - outside * swept, keepdims=True)
     part1[my_plane] = jnp.where(lane == 0, mine, jnp.where(lane == 1, diag_sum, 0.0))
-    finish1, drain1 = share(part1, a1send, a1recv, plane_group, my_plane, plane_peer)
+    finish1, drain1 = share(part1, a1send, a1recv, my_plane, plane_peers)
 
     both = jnp.concatenate([swept, pltpu.roll(swept, SLOT, 1)], 0)
     spread = select_dot(both, gsum[...], 1)
@@ -577,13 +596,13 @@
 
     sweep(3)
     part2[ix] = finish1()
-    finish2, drain2 = share(part2, a2send, a2recv, nx, ix, line_peer)
+    finish2, drain2 = share(part2, a2send, a2recv, ix, line_peers)
 
     sweep(SWEEPS)
 
     for f in range(5):
-        for d in range(6):
-            @pl.when(dirs[d][2])
+        for d in range(8):
+            @pl.when(dirs[d % 6][2])
             def _():
                 fine_copy(f, d).wait_send()
     for q in range(2):
@@ -633,9 +652,9 @@
                 ],
                 pltpu.VMEM((BLOCKS - 2, 6, 3 * RATIO, 128), f32),
                 pltpu.VMEM((ny * nz, 1, 128), f32), pltpu.VMEM((nx, 1, 128), f32),
-                dma((3, 2)), dma((5, 6)), dma((5, 6)),
-                dma((2, 2)), dma((2, 2)), dma((2, BLOCKS)), dma((2, BLOCKS)), dma((2, 2)), dma((2, 2)),
-                dma((ny * nz,)), dma((ny * nz,)), dma((nx,)), dma((nx,)),
+                dma((3, 2)), dma((5, 8)), dma((5, 8)),
+                dma((2, 2)), dma((2, 2)), dma((2, BLOCKS)), dma((2, BLOCKS)), dma((2, 6)), dma((2, 6)),
+                dma((1,)), dma((1,)), dma((1,)), dma((1,)),
             ],
             compiler_params=pltpu.CompilerParams(
                 collective_id=0, has_side_effects=True, vmem_limit_bytes=40 << 20

time: 45.4 us -> 44.1 us (0.971)
  Pallas kernels: 44.4 us -> 43 us
    pallas_call x1, Pallas kernels: 44.4 us -> 43 us  [shards(): pl.pallas_call(body, out_shape=jax.ShapeDtypeStruct((D, R, W), f32), in_s...]
where the time goes in v4:
time: 44.1 us; the launch traced here: 44 us
  Pallas kernels  43 us (98%)
  local copies, waits for them, and re-layouts  0.97 us (2%)
    pallas_call x1, Pallas kernels, shards(): pl.pallas_call(body, out_shape=jax.ShapeDtypeStruct((D, R, W), f32), in_s...  43 us
    unnamed x1, local copies, waits for them, and re-layouts  0.97 us

profile of v4, /device:TPU:1, one launch (start us, length us, event | category | flops | bytes accessed | tf_op | source)
XLA Modules:
  0.0 44.0 jit_solution(10220639371532978006)
XLA Ops:
  0.0 43.0 %shard_map.37 = f32[16,64,256]{2,1,0:T(8,128)S(1)} custom-call(f32[16,64,256]{2,1,0:T(8,128)} %refs_0_.1, f32[16,64,256]{2,1,0:T(8,128)} %refs_1_.1, f32[16,64,256]{2,1,0:T(8,128)} %refs_2_.1), custom_call_target="tpu_custom_call" | custom-call | tf_op jit(solution)/shard_map/pallas_call | solution.py:636
  43.1 1.0 %copy.5 = f32[16,64,256]{2,1,0:T(8,128)} copy(f32[16,64,256]{2,1,0:T(8,128)S(1)} %shard_map.37) | data formatting | bytes 2097152

commit v5 on v4

--- a/solution.py
+++ b/solution.py
@@ -71,10 +71,13 @@
         for h in range(2):
             there = place.at[h, planes, own] if n < 2 else place.at[h]
             loads.append(
-                pltpu.make_async_copy(ref.at[:, :, pl.ds(h * H, H)], there, load_sem.at[n, h])
+                pltpu.make_async_copy(ref.at[:, :, pl.ds(h * H, H)], there, load_sem.at[n])
             )
     for load in loads:
         load.start()
+
+    def loaded(n):
+        pltpu.make_async_copy((k_hbm, p_hbm, s_hbm)[n], out, load_sem.at[n]).wait()
 
     barrier = pltpu.get_barrier_semaphore()
 
@@ -147,8 +150,8 @@
         return pltpu.make_async_remote_copy(
             src_ref=here,
             dst_ref=back if incoming else there,
-            send_sem=fsend.at[f, d + shift],
-            recv_sem=frecv.at[f, (d if incoming else end) + shift],
+            send_sem=fsend.at[f % 2, d + shift],
+            recv_sem=frecv.at[f % 3, (d if incoming else end) + shift],
             device_id={axis: other},
             device_id_type=MESH,
         )
@@ -164,6 +167,8 @@
                 here, there = here.at[pl.ds(0, 1)], there.at[pl.ds(0, 1)]
             sems, to = (czs, czr), {"gx": ix + way}
             sent = REACH + way
+            sent, slot = sent - (sent > REACH), slot - (slot > REACH)
+            first_sem = 2 * REACH * q
         else:
             piece, side = way // 2, way % 2
             axis, other, _ = dirs[(4 if stage == "x" else 2) + side]
@@ -171,14 +176,16 @@
             if stage == "x":
                 here, there, sems = own_q, x_q.at[slot], (cxs, cxr)
             else:
-                first, size = ((REACH - 2, 3), (0, REACH - 2), (REACH + 1, REACH - 2))[piece]
+                pieces = ((REACH - 2, 3), (0, REACH - 2), (REACH + 1, REACH - 2))
+                first, size = pieces[piece] if q == 0 else (0, BLOCKS - 2)
                 here = z_q.at[pl.ds(first + 1, size)]
                 there = y_q.at[slot % 2, pl.ds(first, size)]
                 sems = (cys, cyr)
             to, sent = {axis: other}, way
+            first_sem = (2 if stage == "x" else 6) * q
         return pltpu.make_async_remote_copy(
-            src_ref=here, dst_ref=there, send_sem=sems[0].at[q, sent],
-            recv_sem=sems[1].at[q, slot], device_id=to, device_id_type=MESH,
+            src_ref=here, dst_ref=there, send_sem=sems[0].at[first_sem + sent],
+            recv_sem=sems[1].at[first_sem + slot], device_id=to, device_id_type=MESH,
         )
 
     def ways(q, stage, incoming):
@@ -186,7 +193,7 @@
             useless = (-REACH if incoming else REACH) if q == 0 else 0
             return [(way, exists) for way, exists in far.items() if way != useless]
         first = 4 if stage == "x" else 2
-        return [(way, dirs[first + way % 2][2]) for way in range(2 if stage == "x" else 6)]
+        return [(way, dirs[first + way % 2][2]) for way in range(6 if stage == "y" and q == 0 else 2)]
 
     def coarse_start(q, stage, only=None):
         for way, exists in ways(q, stage, False):
@@ -216,6 +223,8 @@
         for d in which:
             @pl.when(dirs[d % 6][2])
             def _():
+                if f >= 2:
+                    make(f - 2, d).wait_send()
                 make(f, d).start()
 
     def arrive(make, f, which):
@@ -281,15 +290,13 @@
             mine = lax.rem(lane, 16) // 4 == i
             return tuple(jnp.where(mine, pltpu.roll(a, z, 1), b) for a, b in zip(fresh, faces))
 
-        return lax.fori_loop(0, D // 4, pack, (zero_tile, zero_tile))
-
-    for load in loads[:2]:
-        load.wait()
+        return lax.fori_loop(0, D // 4, pack, (zero_tile, zero_tile), unroll=2)
+
+    loaded(0)
     keep_packed(KF, pack_field(kx))
     pl.semaphore_wait(barrier, near + (plane_group - 1) + (nx - 1))
     start(fine_copy, KF, (4, 5, 2, 3, 0, 1, 6, 7))
-    for load in loads[2:4]:
-        load.wait()
+    loaded(1)
     keep_packed(1, pack_field(p0))
     start(fine_copy, 1, (4, 5, 2, 3, 0, 1, 6, 7))
 
@@ -416,8 +423,7 @@
         merge(0)
         coarse_start(0, "z")
 
-    loads[4].wait()
-    loads[5].wait()
+    loaded(2)
 
     def sweep_planes(n, base, offsets, faces, part=range(R // GROUP)):
         field = press[n - 1]
@@ -510,9 +516,10 @@
     def turn_to_y(q):
         near_z = (-1, 1)
         coarse_arrive(q, "z", near_z)
-        coarse_start(q, "y", (0, 1))
+        if q == 0:
+            coarse_start(q, "y", (0, 1))
         coarse_arrive(q, "z", [dz for dz in far if dz not in near_z])
-        coarse_start(q, "y", (2, 3, 4, 5))
+        coarse_start(q, "y", (2, 3, 4, 5) if q == 0 else (0, 1))
 
     turn_to_y(0)
     sweep(2, lambda: turn_to_y(1))
@@ -600,7 +607,7 @@
 
     sweep(SWEEPS)
 
-    for f in range(5):
+    for f in (3, 4):
         for d in range(8):
             @pl.when(dirs[d % 6][2])
             def _():
@@ -652,8 +659,8 @@
                 ],
                 pltpu.VMEM((BLOCKS - 2, 6, 3 * RATIO, 128), f32),
                 pltpu.VMEM((ny * nz, 1, 128), f32), pltpu.VMEM((nx, 1, 128), f32),
-                dma((3, 2)), dma((5, 8)), dma((5, 8)),
-                dma((2, 2)), dma((2, 2)), dma((2, BLOCKS)), dma((2, BLOCKS)), dma((2, 6)), dma((2, 6)),
+                dma((3,)), dma((2, 8)), dma((3, 8)),
+                dma((4,)), dma((4,)), dma((4 * REACH,)), dma((4 * REACH,)), dma((8,)), dma((8,)),
                 dma((1,)), dma((1,)), dma((1,)), dma((1,)),
             ],
             compiler_params=pltpu.CompilerParams(

time: 44.1 us -> 43.9 us (level)
  no operation moved by 1% of the time
where the time goes in v5:
time: 43.9 us; the launch traced here: 43.8 us
  Pallas kernels  42.8 us (97%)
  local copies, waits for them, and re-layouts  0.97 us (2%)
    pallas_call x1, Pallas kernels, shards(): pl.pallas_call(body, out_shape=jax.ShapeDtypeStruct((D, R, W), f32), in_s...  42.8 us
    unnamed x1, local copies, waits for them, and re-layouts  0.97 us

profile of v5, /device:TPU:1, one launch (start us, length us, event | category | flops | bytes accessed | tf_op | source)
XLA Modules:
  0.0 43.8 jit_solution(10534039701299442790)
XLA Ops:
  0.0 42.8 %shard_map.37 = f32[16,64,256]{2,1,0:T(8,128)S(1)} custom-call(f32[16,64,256]{2,1,0:T(8,128)} %refs_0_.1, f32[16,64,256]{2,1,0:T(8,128)} %refs_1_.1, f32[16,64,256]{2,1,0:T(8,128)} %refs_2_.1), custom_call_target="tpu_custom_call" | custom-call | tf_op jit(solution)/shard_map/pallas_call | solution.py:643
  42.8 1.0 %copy.5 = f32[16,64,256]{2,1,0:T(8,128)} copy(f32[16,64,256]{2,1,0:T(8,128)S(1)} %shard_map.37) | data formatting | bytes 2097152

commit v6 on v5

--- a/solution.py
+++ b/solution.py
@@ -23,6 +23,7 @@
 REACH = 4
 BLOCKS = 2 * REACH + 1
 KF = 0
+PAUSE = 4
 CHUNK = R // 2
 GROUP = 16
 
@@ -470,7 +471,7 @@
     none = (zero_tile, zero_tile)
     rim = (0, D - 1)
 
-    def sweep(n, between=lambda: None):
+    def sweep(n, between=None):
         def inner(i, faces):
             return sweep_planes(n, 2 * i + 1, (0, 1), faces)
 
@@ -487,8 +488,12 @@
         if n < SWEEPS:
             faces = lax.fori_loop(0, 1, inner, faces)
             start(fine_copy, n + 1, (0, 1))
-        faces = lax.fori_loop(1 if n < SWEEPS else 0, count, inner, faces)
-        between()
+        middle = 1 if n < SWEEPS else 0
+        if between is not None:
+            faces = lax.fori_loop(middle, PAUSE, inner, faces)
+            between()
+            middle = PAUSE
+        faces = lax.fori_loop(middle, count, inner, faces)
         arrive(fine_copy, n, (6, 7))
         faces = sweep_planes(n, 0, rim, faces, second)
         if n < SWEEPS:
@@ -505,9 +510,8 @@
 
     own_f[0] = fixed
     coarse_start(1, "x")
-    start(fine_copy, 2, (2, 3, 0, 1))
     keep_packed(2, pack_field(p1))
-    start(fine_copy, 2, (4, 5, 6, 7))
+    start(fine_copy, 2, (4, 5, 2, 3, 0, 1, 6, 7))
     push_weights()
 
     coarse_arrive(1, "x")

time: 43.9 us -> 42.4 us (0.966)
  Pallas kernels: 42.8 us -> 41.2 us
    pallas_call x1, Pallas kernels: 42.8 us -> 41.2 us  [shards(): pl.pallas_call(body, out_shape=jax.ShapeDtypeStruct((D, R, W), f32), in_s...]
where the time goes in v6:
time: 42.4 us; the launch traced here: 42.2 us
  Pallas kernels  41.2 us (97%)
  local copies, waits for them, and re-layouts  0.97 us (2%)
    pallas_call x1, Pallas kernels, shards(): pl.pallas_call(body, out_shape=jax.ShapeDtypeStruct((D, R, W), f32), in_s...  41.2 us
    unnamed x1, local copies, waits for them, and re-layouts  0.97 us

profile of v6, /device:TPU:1, one launch (start us, length us, event | category | flops | bytes accessed | tf_op | source)
XLA Modules:
  0.0 42.2 jit_solution(5187495418441747046)
XLA Ops:
  0.0 41.2 %shard_map.37 = f32[16,64,256]{2,1,0:T(8,128)S(1)} custom-call(f32[16,64,256]{2,1,0:T(8,128)} %refs_0_.1, f32[16,64,256]{2,1,0:T(8,128)} %refs_1_.1, f32[16,64,256]{2,1,0:T(8,128)} %refs_2_.1), custom_call_target="tpu_custom_call" | custom-call | tf_op jit(solution)/shard_map/pallas_call | solution.py:647
  41.2 1.0 %copy.5 = f32[16,64,256]{2,1,0:T(8,128)} copy(f32[16,64,256]{2,1,0:T(8,128)S(1)} %shard_map.37) | data formatting | bytes 2097152

commit v7 on v6

--- a/solution.py
+++ b/solution.py
@@ -291,7 +291,7 @@
             mine = lax.rem(lane, 16) // 4 == i
             return tuple(jnp.where(mine, pltpu.roll(a, z, 1), b) for a, b in zip(fresh, faces))
 
-        return lax.fori_loop(0, D // 4, pack, (zero_tile, zero_tile), unroll=2)
+        return lax.fori_loop(0, D // 4, pack, (zero_tile, zero_tile), unroll=4)
 
     loaded(0)
     keep_packed(KF, pack_field(kx))
@@ -478,7 +478,7 @@
         count = D // 2 - 1
         if n == 1:
             arrive(fine_copy, n, range(2, 6))
-            lax.fori_loop(0, count, inner, none)
+            lax.fori_loop(0, count, inner, none, unroll=count)
             arrive(fine_copy, n, (0, 1, 6, 7))
             sweep_planes(n, 0, rim, none)
             return

time: 42.4 us -> 42.1 us (level)
  no operation moved by 1% of the time
where the time goes in v7:
time: 42.1 us; the launch traced here: 42 us
  Pallas kernels  41 us (97%)
  local copies, waits for them, and re-layouts  0.97 us (2%)
    pallas_call x1, Pallas kernels, shards(): pl.pallas_call(body, out_shape=jax.ShapeDtypeStruct((D, R, W), f32), in_s...  41 us
    unnamed x1, local copies, waits for them, and re-layouts  0.97 us

profile of v7, /device:TPU:1, one launch (start us, length us, event | category | flops | bytes accessed | tf_op | source)
XLA Modules:
  0.0 42.0 jit_solution(7693793844986240355)
XLA Ops:
  0.0 41.0 %shard_map.37 = f32[16,64,256]{2,1,0:T(8,128)S(1)} custom-call(f32[16,64,256]{2,1,0:T(8,128)} %refs_0_.1, f32[16,64,256]{2,1,0:T(8,128)} %refs_1_.1, f32[16,64,256]{2,1,0:T(8,128)} %refs_2_.1), custom_call_target="tpu_custom_call" | custom-call | tf_op jit(solution)/shard_map/pallas_call | solution.py:647
  41.0 1.0 %copy.5 = f32[16,64,256]{2,1,0:T(8,128)} copy(f32[16,64,256]{2,1,0:T(8,128)S(1)} %shard_map.37) | data formatting | bytes 2097152
